TPU v7x, 512 devices: a whole 4x8x8 slice. The times are simulated.
512 devices in a mesh: sec: 4 (over z_lo), gx: 8 (over z_hi, x), gy: 16 (over y, core).
Axes of the slice: x: 4, y: 8, z: 8 (z_hi: 2, z_lo: 4; z = z_hi * 4 + z_lo), core: 2. Of those that a mesh axis runs over, the one named last changes fastest.
Arguments:
- soil_class: int32 [256, 4096], P('gx', 'gy'), may hold values from 0 to 11
- geology_class: int32 [256, 4096], P('gx', 'gy'), may hold values from 0 to 15
- land_mask: int32 [256, 4096], P('gx', 'gy'), may hold values 0 or 1
- river_mask: int32 [256, 4096], P('gx', 'gy'), may hold values 0 or 1
- elevation: float32 [256, 4096], P('gx', 'gy'), may hold values from -6 to 6
- roughness: float32 [256, 4096], P('gx', 'gy'), may hold values from 0.02 to 0.11
- rainfall: float32 [256, 4096], P('gx', 'gy'), may hold values from 0.05 to 1
- potential_evap: float32 [256, 4096], P('gx', 'gy'), may hold values from 0.05 to 0.5
- surface_head: float32 [256, 4096], P('gx', 'gy'), may hold values from -3 to 3
- pressure: float32 [8, 256, 4096], P('sec', 'gx', 'gy'), may hold values from -6 to 6
- storage: float32 [8, 256, 4096], P('sec', 'gx', 'gy'), may hold values from 0.2 to 2
- soil_embed: bfloat16 [12, 128], replicated, may hold values from -4 to 4
- geology_embed: bfloat16 [16, 128], replicated, may hold values from -4 to 4
- conv_weight: bfloat16 [3, 3, 128, 128], replicated, may hold values from -0.1875 to 0.1875
- out_weight: bfloat16 [128, 8], replicated, may hold values from -0.5 to 0.5
Outputs:
- pressure_out: float32 [8, 256, 4096], P('sec', 'gx', 'gy')
- head_out: float32 [256, 4096], P('gx', 'gy')
All inputs are finite; a program needn't handle non-finite values. No bound on the sum of `land_mask` or of `river_mask` on one device may be relied on, other than what follows from the above.
Results may differ from a plain program's by a relative error of at most 0.0041.
Values sent between devices are 32-bit elements; how exact they have to be, the bound alone decides.
No kernel may reach another device: no remote copies, remote signals or barrier semaphores. Data moves between devices by JAX's collectives and lax.ppermute only.
A program may use at most 64 MiB of HBM per device.

v0:
```python
import jax
import jax.numpy as jnp
from jax import lax
from jax.sharding import PartitionSpec as P

SWEEPS = 4
CYCLES = 4
infil_rate = 0.3
lateral = 1.0
vertical = 0.5


def padded(block, sides, width):
    for axis, dim in sides:
        count = lax.axis_size(axis)
        forward = [(i, i + 1) for i in range(count - 1)]
        backward = [(target, source) for source, target in forward]
        low = lax.ppermute(
            lax.slice_in_dim(block, block.shape[dim] - width, None, axis=dim), axis, forward
        )
        high = lax.ppermute(lax.slice_in_dim(block, 0, width, axis=dim), axis, backward)
        block = jnp.concatenate([low, block, high], axis=dim)
    return block


def spread(value, axis, root):
    mine = lax.axis_index(axis) == root
    return lax.psum(jnp.where(mine, value, jnp.zeros_like(value)), axis)


def infiltration(land_frac, top_cond, surface, top_press):
    return land_frac * (infil_rate * top_cond / (1.0 + top_cond)) * (surface - top_press)


def evaporation_loss(land_frac, potential, top_press):
    return land_frac * potential * jax.nn.sigmoid(top_press)


def surface_flux(level_pad, rough_pad):
    centre_level = level_pad[1:-1, 1:-1]
    centre_rough = rough_pad[1:-1, 1:-1]
    total = jnp.zeros_like(centre_level)
    pairs = (
        (level_pad[2:, 1:-1], rough_pad[2:, 1:-1]),
        (level_pad[:-2, 1:-1], rough_pad[:-2, 1:-1]),
        (level_pad[1:-1, 2:], rough_pad[1:-1, 2:]),
        (level_pad[1:-1, :-2], rough_pad[1:-1, :-2]),
    )
    for near_level, near_rough in pairs:
        total = total + 0.5 * (centre_rough + near_rough) * (near_level - centre_level)
    return total


def shifted(values):
    return [
        (values[:-2, 1:-1, 1:-1], vertical),
        (values[2:, 1:-1, 1:-1], vertical),
        (values[1:-1, :-2, 1:-1], lateral),
        (values[1:-1, 2:, 1:-1], lateral),
        (values[1:-1, 1:-1, 2:], lateral),
        (values[1:-1, 1:-1, :-2], lateral),
    ]


def jacobi_sweep(press_pad, cond_pad, rhs_mid, store_mid):
    cond_mid = cond_pad[1:-1, 1:-1, 1:-1]
    diagonal = store_mid
    total = rhs_mid
    for (near_press, factor), (near_cond, unused) in zip(shifted(press_pad), shifted(cond_pad)):
        face = factor * 0.5 * (cond_mid + near_cond)
        diagonal = diagonal + face
        total = total + face * near_press
    return total / diagonal


def tile_features(soil_class, geology_class, soil_embed, geology_embed):
    soil_onehot = (
        soil_class[:, :, None] == jnp.arange(soil_embed.shape[0], dtype=jnp.int32)
    ).astype(jnp.bfloat16)
    geology_onehot = (
        geology_class[:, :, None] == jnp.arange(geology_embed.shape[0], dtype=jnp.int32)
    ).astype(jnp.bfloat16)
    total = jnp.einsum("xys,sc->xyc", soil_onehot, soil_embed, preferred_element_type=jnp.float32)
    total = total + jnp.einsum(
        "xys,sc->xyc", geology_onehot, geology_embed, preferred_element_type=jnp.float32
    )
    return total.astype(jnp.bfloat16)


def conv_relu(features_pad, kernel):
    convolved = lax.conv_general_dilated(
        features_pad[None],
        kernel,
        (1, 1),
        "VALID",
        dimension_numbers=("NHWC", "HWIO", "NCHW"),
        preferred_element_type=jnp.float32,
    )[0]
    return jax.nn.relu(convolved).astype(jnp.bfloat16)


def shards(
    soil_class,
    geology_class,
    land_mask,
    river_mask,
    elevation,
    roughness,
    rainfall,
    potential_evap,
    surface_head,
    pressure,
    storage,
    soil_embed,
    geology_embed,
    conv_weight,
    out_weight,
):
    sec_count = lax.axis_size("sec")
    sec_index = lax.axis_index("sec")
    layers_dev, tile_rows, tile_cols = pressure.shape
    class_pad = (
        padded(jnp.stack((soil_class + 1, geology_class + 1)), (("gx", 1), ("gy", 2)), 1) - 1
    )
    features_pad = tile_features(class_pad[0], class_pad[1], soil_embed, geology_embed)
    hidden = conv_relu(features_pad, conv_weight)
    own_out = lax.dynamic_slice_in_dim(out_weight, sec_index * layers_dev, layers_dev, 1)
    logits = jnp.einsum("cxy,cl->lxy", hidden, own_out, preferred_element_type=jnp.float32)
    conduct = jnp.exp(logits)
    depth = 1
    coeff_pad = padded(jnp.stack((conduct, storage)), (("sec", 1), ("gx", 2), ("gy", 3)), depth)
    cond_pad = coeff_pad[0]
    top_cond = spread(conduct[0], "sec", 0)
    land_frac = land_mask.astype(jnp.float32)
    river_frac = river_mask.astype(jnp.float32)
    rough = land_frac * (1.0 + river_frac) * roughness
    rough_pad = padded(rough, (("gx", 0), ("gy", 1)), 1)
    strip_rows = tile_rows // sec_count
    first_row = sec_index * strip_rows

    def strip_of(values):
        return lax.dynamic_slice_in_dim(values, first_row, strip_rows, 0)

    strip_land = strip_of(land_frac)
    strip_rain = strip_of(rainfall)
    strip_potential = strip_of(potential_evap)
    strip_cond = strip_of(top_cond)
    strip_rough = lax.dynamic_slice_in_dim(rough_pad, first_row, strip_rows + 2, 0)
    layer_ids = sec_index * layers_dev + jnp.arange(layers_dev, dtype=jnp.int32)
    top_layer = (layer_ids == 0).astype(jnp.float32)[:, None, None]
    surface = surface_head
    press = pressure
    for cycle in range(CYCLES):
        top_press = spread(press[0], "sec", 0)
        level_pad = padded(surface + elevation, (("gx", 0), ("gy", 1)), 1)
        level_strip = lax.dynamic_slice_in_dim(level_pad, first_row, strip_rows + 2, 0)
        flux = surface_flux(level_strip, strip_rough)
        old_strip = strip_of(surface)
        top_strip = strip_of(top_press)
        infil = infiltration(strip_land, strip_cond, old_strip, top_strip)
        evap = evaporation_loss(strip_land, strip_potential, top_strip)
        new_strip = old_strip + strip_land * (strip_rain - infil + flux)
        source_strip = infil - evap
        surface, source = (
            lax.all_gather(new_strip, "sec", axis=0, tiled=True),
            lax.all_gather(source_strip, "sec", axis=0, tiled=True),
        )
        rhs = storage * press + top_layer * source[None]
        for sweep in range(SWEEPS):
            press_pad = padded(press, (("sec", 0), ("gx", 1), ("gy", 2)), 1)
            press = jacobi_sweep(press_pad, cond_pad, rhs, storage)
    return (press, surface)


def solution(mesh):
    in_specs = (
        P("gx", "gy"),
        P("gx", "gy"),
        P("gx", "gy"),
        P("gx", "gy"),
        P("gx", "gy"),
        P("gx", "gy"),
        P("gx", "gy"),
        P("gx", "gy"),
        P("gx", "gy"),
        P("sec", "gx", "gy"),
        P("sec", "gx", "gy"),
        P(),
        P(),
        P(),
        P(),
    )
    out_specs = (P("sec", "gx", "gy"), P("gx", "gy"))
    return jax.shard_map(shards, mesh=mesh, in_specs=in_specs, out_specs=out_specs, check_vma=False)
```

profile of v0, /device:TPU:38, one launch (start us, length us, event | category | flops | bytes accessed | tf_op | source)
XLA Modules:
  0.0 819.4 jit_solution(7540490617223454841)
XLA Ops:
  8.0 10.8 %collective-permute-start = (s32[2,1,256]{2,1,0:T(1,128)S(1)}, s32[2,1,256]{2,1,0:T(1,128)S(1)}, u32[]{:S(2)}, u32[]{:S(2)}) collective-permute-start(s32[2,1,256]{2,1,0:T(1,128)S(1)} %get-tuple-element.138), channel_id=1, source_target_pairs={{0,16},{16,32},{32,48},{48,64},{64,80},{80,96},{96,112},{1,17},{17... | collective-permute-start | bytes 6152 | tf_op jit(solution)/shard_map/ppermute | solution.py:18
  21.6 9.9 %collective-permute-start.38 = (f32[1,256]{1,0:T(1,128)S(1)}, f32[1,256]{1,0:T(1,128)S(1)}, u32[]{:S(2)}, u32[]{:S(2)}) collective-permute-start(f32[1,256]{1,0:T(1,128)S(1)} %get-tuple-element.161), channel_id=1, source_target_pairs={{0,16},{16,32},{32,48},{48,64},{64,80},{80,96},{96,112},{1,17},{17... | collective-permute-start | bytes 3080 | tf_op jit(solution)/shard_map/ppermute | solution.py:18
  34.3 9.9 %collective-permute-start.34 = (f32[1,256]{1,0:T(1,128)S(1)}, f32[1,256]{1,0:T(1,128)S(1)}, u32[]{:S(2)}, u32[]{:S(2)}) collective-permute-start(f32[1,256]{1,0:T(1,128)S(1)} %get-tuple-element.159), channel_id=1, source_target_pairs={{0,16},{16,32},{32,48},{48,64},{64,80},{80,96},{96,112},{1,17},{17... | collective-permute-start | bytes 3080 | tf_op jit(solution)/shard_map/ppermute | solution.py:18
  53.8 4.1 collective-permute-done.35
  70.2 4.9 collective-permute-start.3
  86.2 5.4 maximum_convert_fusion
  98.5 8.8 %collective-permute-start.12 = (f32[4,1,256]{2,1,0:T(1,128)S(1)}, f32[4,1,256]{2,1,0:T(1,128)S(1)}, u32[]{:S(2)}, u32[]{:S(2)}) collective-permute-start(f32[4,1,256]{2,1,0:T(1,128)S(1)} %get-tuple-element.91), channel_id=1, source_target_pairs={{0,16},{16,32},{32,48},{48,64},{64,80},{80,96},{96,112},{1,17},{17... | collective-permute-start | bytes 12296 | tf_op jit(solution)/shard_map/ppermute | solution.py:18
  109.2 4.5 collective-permute-start.4
  124.3 6.8 collective-permute-start.6
  133.1 38.9 %all-reduce.3.cloned.1.call-done = (f32[32,256]{1,0:T(8,128)}, f32[32,256]{1,0:T(8,128)}) async-done(((f32[32,256]{1,0:T(8,128)}, f32[32,256]{1,0:T(8,128)}), (f32[32,256]{1,0:T(8,128)}, f32[32,256]{1,0:T(8,128)})) %all-reduce.3.cloned.1.call-update) | async-done | bytes 65552 | tf_op jit(solution)/shard_map/psum | solution.py:28
  175.7 4.9 collective-permute-start.9
  180.6 13.1 %all_gather.24 = f32[32,256]{1,0:T(8,128)S(1)} all-gather(f32[8,256]{1,0:T(8,128)S(1)} %get-tuple-element.21), channel_id=1, replica_groups=mesh['sec'=4,'gx'=8,'gy'=16] {'sec'}, dimensions={0}, use_global_device_ids=true | all-gather | bytes 40960 | tf_op jit(solution)/shard_map/all_gather | solution.py:166
  197.0 4.2 collective-permute-done.17
  201.3 6.9 collective-permute-start.18
  210.1 9.6 %collective-permute-done.19 = f32[4,1,256]{2,1,0:T(1,128)S(1)} collective-permute-done((f32[4,1,256]{2,1,0:T(1,128)S(1)}, f32[4,1,256]{2,1,0:T(1,128)S(1)}, u32[]{:S(2)}, u32[]{:S(2)}) %collective-permute-start.19) | collective-permute-done | bytes 4128 | tf_op jit(solution)/shard_map/ppermute | solution.py:21
  224.1 4.5 collective-permute-done.21
  233.2 4.3 collective-permute-done.23
  243.4 13.1 %all_gather.25 = f32[32,256]{1,0:T(8,128)S(1)} all-gather(f32[8,256]{1,0:T(8,128)S(1)} %get-tuple-element.8), channel_id=1, replica_groups=mesh['sec'=4,'gx'=8,'gy'=16] {'sec'}, dimensions={0}, use_global_device_ids=true | all-gather | bytes 40960 | tf_op jit(solution)/shard_map/all_gather | solution.py:165
  261.0 7.9 collective-permute-start.66
  274.7 5.8 collective-permute-done.67
  280.5 8.6 %collective-permute-start.30 = (f32[4,1,256]{2,1,0:T(1,128)S(1)}, f32[4,1,256]{2,1,0:T(1,128)S(1)}, u32[]{:S(2)}, u32[]{:S(2)}) collective-permute-start(f32[4,1,256]{2,1,0:T(1,128)S(1)} %get-tuple-element.83), channel_id=1, source_target_pairs={{0,16},{16,32},{32,48},{48,64},{64,80},{80,96},{96,112},{1,17},{17... | collective-permute-start | bytes 12296 | tf_op jit(solution)/shard_map/ppermute | solution.py:18
  293.1 4.9 collective-permute-start.69
  305.3 4.4 collective-permute-done.33
  314.0 19.2 %psum.37 = f32[32,256]{1,0:T(8,128)S(1)} all-reduce(f32[32,256]{1,0:T(8,128)S(1)} %get-tuple-element.127), channel_id=1, replica_groups=mesh['sec'=4,'gx'=8,'gy'=16] {'sec'}, use_global_device_ids=true, to_apply=%region_2.3 | all-reduce | flops 8192 | bytes 65536 | tf_op jit(solution)/shard_map/psum | solution.py:28
  333.2 7.2 collective-permute-start.44
  342.5 9.5 %collective-permute-done.45 = f32[4,1,256]{2,1,0:T(1,128)S(1)} collective-permute-done((f32[4,1,256]{2,1,0:T(1,128)S(1)}, f32[4,1,256]{2,1,0:T(1,128)S(1)}, u32[]{:S(2)}, u32[]{:S(2)}) %collective-permute-start.45) | collective-permute-done | bytes 4128 | tf_op jit(solution)/shard_map/ppermute | solution.py:21
  356.4 13.2 %all_gather.26 = f32[32,256]{1,0:T(8,128)S(1)} all-gather(f32[8,256]{1,0:T(8,128)S(1)} %get-tuple-element.102), channel_id=1, replica_groups=mesh['sec'=4,'gx'=8,'gy'=16] {'sec'}, dimensions={0}, use_global_device_ids=true | all-gather | bytes 40960 | tf_op jit(solution)/shard_map/all_gather | solution.py:166
  372.6 4.2 collective-permute-done.49
  382.7 7.6 collective-permute-done.51
  394.8 4.5 collective-permute-done.53
  404.7 4.2 collective-permute-done.55
  414.8 13.1 %all_gather.27 = f32[32,256]{1,0:T(8,128)S(1)} all-gather(f32[8,256]{1,0:T(8,128)S(1)} %get-tuple-element.101), channel_id=1, replica_groups=mesh['sec'=4,'gx'=8,'gy'=16] {'sec'}, dimensions={0}, use_global_device_ids=true | all-gather | bytes 40960 | tf_op jit(solution)/shard_map/all_gather | solution.py:165
  432.4 7.9 collective-permute-start.94
  445.1 6.8 collective-permute-done.95
  451.9 7.6 collective-permute-start.62
  463.5 4.9 collective-permute-start.97
  475.7 4.4 collective-permute-done.65
  485.2 18.3 %psum.38 = f32[32,256]{1,0:T(8,128)S(1)} all-reduce(f32[32,256]{1,0:T(8,128)S(1)} %get-tuple-element.118), channel_id=1, replica_groups=mesh['sec'=4,'gx'=8,'gy'=16] {'sec'}, use_global_device_ids=true, to_apply=%region_3.4 | all-reduce | flops 8192 | bytes 65536 | tf_op jit(solution)/shard_map/psum | solution.py:28
  503.6 7.2 collective-permute-start.72
  512.8 9.5 %collective-permute-done.73 = f32[4,1,256]{2,1,0:T(1,128)S(1)} collective-permute-done((f32[4,1,256]{2,1,0:T(1,128)S(1)}, f32[4,1,256]{2,1,0:T(1,128)S(1)}, u32[]{:S(2)}, u32[]{:S(2)}) %collective-permute-start.73) | collective-permute-done | bytes 4128 | tf_op jit(solution)/shard_map/ppermute | solution.py:21
  526.8 13.2 %all_gather.28 = f32[32,256]{1,0:T(8,128)S(1)} all-gather(f32[8,256]{1,0:T(8,128)S(1)} %get-tuple-element.100), channel_id=1, replica_groups=mesh['sec'=4,'gx'=8,'gy'=16] {'sec'}, dimensions={0}, use_global_device_ids=true | all-gather | bytes 40960 | tf_op jit(solution)/shard_map/all_gather | solution.py:166
  543.0 4.2 collective-permute-done.77
  553.1 7.6 collective-permute-done.79
  565.1 4.5 collective-permute-done.81
  575.1 4.2 collective-permute-done.83
  585.2 13.1 %all_gather.29 = f32[32,256]{1,0:T(8,128)S(1)} all-gather(f32[8,256]{1,0:T(8,128)S(1)} %get-tuple-element.99), channel_id=1, replica_groups=mesh['sec'=4,'gx'=8,'gy'=16] {'sec'}, dimensions={0}, use_global_device_ids=true | all-gather | bytes 40960 | tf_op jit(solution)/shard_map/all_gather | solution.py:165
  602.8 7.9 collective-permute-start.122
  615.5 6.8 collective-permute-done.123
  622.3 7.6 collective-permute-start.90
  633.8 4.9 collective-permute-start.125
  646.0 4.4 collective-permute-done.93
  655.6 18.3 %psum.39 = f32[32,256]{1,0:T(8,128)S(1)} all-reduce(f32[32,256]{1,0:T(8,128)S(1)} %get-tuple-element.109), channel_id=1, replica_groups=mesh['sec'=4,'gx'=8,'gy'=16] {'sec'}, use_global_device_ids=true, to_apply=%region_4.5 | all-reduce | flops 8192 | bytes 65536 | tf_op jit(solution)/shard_map/psum | solution.py:28
  673.9 7.2 collective-permute-start.100
  683.2 9.5 %collective-permute-done.101 = f32[4,1,256]{2,1,0:T(1,128)S(1)} collective-permute-done((f32[4,1,256]{2,1,0:T(1,128)S(1)}, f32[4,1,256]{2,1,0:T(1,128)S(1)}, u32[]{:S(2)}, u32[]{:S(2)}) %collective-permute-start.101) | collective-permute-done | bytes 4128 | tf_op jit(solution)/shard_map/ppermute | solution.py:21
  697.2 13.2 %all_gather.30 = f32[32,256]{1,0:T(8,128)S(1)} all-gather(f32[8,256]{1,0:T(8,128)S(1)} %get-tuple-element.98), channel_id=1, replica_groups=mesh['sec'=4,'gx'=8,'gy'=16] {'sec'}, dimensions={0}, use_global_device_ids=true | all-gather | bytes 40960 | tf_op jit(solution)/shard_map/all_gather | solution.py:166
  713.4 4.2 collective-permute-done.105
  723.5 7.6 collective-permute-done.107
  735.5 4.5 collective-permute-done.109
  745.5 4.2 collective-permute-done.111
  755.6 7.6 collective-permute-done.113
  767.6 4.5 collective-permute-done.115
  775.8 4.2 collective-permute-done.117
  785.9 7.6 collective-permute-done.119
  797.9 13.2 %all_gather.31 = f32[32,256]{1,0:T(8,128)S(1)} all-gather(f32[8,256]{1,0:T(8,128)S(1)} %get-tuple-element.97), channel_id=1, replica_groups=mesh['sec'=4,'gx'=8,'gy'=16] {'sec'}, dimensions={0}, use_global_device_ids=true | all-gather | bytes 40960 | tf_op jit(solution)/shard_map/all_gather | solution.py:165
  (358 shorter events, 272.9 us)
Async XLA Ops:
  7.2 164.8 %all-reduce.3.cloned.1.call-start = ((), (), s32[]{:S(2)}) async-start(), calls=%async_computation | async-start | bytes 131072 | tf_op jit(solution)/shard_map/psum | solution.py:28
  8.0 56.0 %collective-permute-start = (s32[2,1,256]{2,1,0:T(1,128)S(1)}, s32[2,1,256]{2,1,0:T(1,128)S(1)}, u32[]{:S(2)}, u32[]{:S(2)}) collective-permute-start(s32[2,1,256]{2,1,0:T(1,128)S(1)} %get-tuple-element.138), channel_id=1, source_target_pairs={{0,16},{16,32},{32,48},{48,64},{64,80},{80,96},{96,112},{1,17},{17... | collective-permute-start | bytes 6152 | tf_op jit(solution)/shard_map/ppermute | solution.py:18
  18.9 49.3 %collective-permute-start.1 = (s32[2,1,256]{2,1,0:T(1,128)S(1)}, s32[2,1,256]{2,1,0:T(1,128)S(1)}, u32[]{:S(2)}, u32[]{:S(2)}) collective-permute-start(s32[2,1,256]{2,1,0:T(1,128)S(1)} %get-tuple-element.139), channel_id=1, source_target_pairs={{16,0},{32,16},{48,32},{64,48},{80,64},{96,80},{112,96},{17,1},{33... | collective-permute-start | bytes 6152 | tf_op jit(solution)/shard_map/ppermute | solution.py:21
  21.6 24.8 %collective-permute-start.38 = (f32[1,256]{1,0:T(1,128)S(1)}, f32[1,256]{1,0:T(1,128)S(1)}, u32[]{:S(2)}, u32[]{:S(2)}) collective-permute-start(f32[1,256]{1,0:T(1,128)S(1)} %get-tuple-element.161), channel_id=1, source_target_pairs={{0,16},{16,32},{32,48},{48,64},{64,80},{80,96},{96,112},{1,17},{17... | collective-permute-start | bytes 3080 | tf_op jit(solution)/shard_map/ppermute | solution.py:18
  31.6 16.8 %collective-permute-start.39 = (f32[1,256]{1,0:T(1,128)S(1)}, f32[1,256]{1,0:T(1,128)S(1)}, u32[]{:S(2)}, u32[]{:S(2)}) collective-permute-start(f32[1,256]{1,0:T(1,128)S(1)} %get-tuple-element.162), channel_id=1, source_target_pairs={{16,0},{32,16},{48,32},{64,48},{80,64},{96,80},{112,96},{17,1},{33... | collective-permute-start | bytes 3080 | tf_op jit(solution)/shard_map/ppermute | solution.py:21
  34.3 17.5 %collective-permute-start.34 = (f32[1,256]{1,0:T(1,128)S(1)}, f32[1,256]{1,0:T(1,128)S(1)}, u32[]{:S(2)}, u32[]{:S(2)}) collective-permute-start(f32[1,256]{1,0:T(1,128)S(1)} %get-tuple-element.159), channel_id=1, source_target_pairs={{0,16},{16,32},{32,48},{48,64},{64,80},{80,96},{96,112},{1,17},{17... | collective-permute-start | bytes 3080 | tf_op jit(solution)/shard_map/ppermute | solution.py:18
  48.3 50.1 %collective-permute-start.10 = (f32[1,32,256]{2,1,0:T(8,128)S(1)}, f32[1,32,256]{2,1,0:T(8,128)S(1)}, u32[]{:S(2)}, u32[]{:S(2)}) collective-permute-start(f32[1,32,256]{2,1,0:T(8,128)S(1)} %get-tuple-element.141), channel_id=1, source_target_pairs={{0,128},{128,256},{256,384},{1,129},{129,257},{257,385},{2,130},{1... | collective-permute-start | bytes 98312 | tf_op jit(solution)/shard_map/ppermute | solution.py:18
  59.9 38.6 %collective-permute-start.11 = (f32[1,32,256]{2,1,0:T(8,128)S(1)}, f32[1,32,256]{2,1,0:T(8,128)S(1)}, u32[]{:S(2)}, u32[]{:S(2)}) collective-permute-start(f32[1,32,256]{2,1,0:T(8,128)S(1)} %get-tuple-element.142), channel_id=1, source_target_pairs={{128,0},{256,128},{384,256},{129,1},{257,129},{385,257},{130,2},{2... | collective-permute-start | bytes 98312 | tf_op jit(solution)/shard_map/ppermute | solution.py:21
  98.5 16.6 %collective-permute-start.12 = (f32[4,1,256]{2,1,0:T(1,128)S(1)}, f32[4,1,256]{2,1,0:T(1,128)S(1)}, u32[]{:S(2)}, u32[]{:S(2)}) collective-permute-start(f32[4,1,256]{2,1,0:T(1,128)S(1)} %get-tuple-element.91), channel_id=1, source_target_pairs={{0,16},{16,32},{32,48},{48,64},{64,80},{80,96},{96,112},{1,17},{17... | collective-permute-start | bytes 12296 | tf_op jit(solution)/shard_map/ppermute | solution.py:18
  107.3 11.5 %collective-permute-start.13 = (f32[4,1,256]{2,1,0:T(1,128)S(1)}, f32[4,1,256]{2,1,0:T(1,128)S(1)}, u32[]{:S(2)}, u32[]{:S(2)}) collective-permute-start(f32[4,1,256]{2,1,0:T(1,128)S(1)} %get-tuple-element.92), channel_id=1, source_target_pairs={{16,0},{32,16},{48,32},{64,48},{80,64},{96,80},{112,96},{17,1},{33... | collective-permute-start | bytes 12296 | tf_op jit(solution)/shard_map/ppermute | solution.py:21
  109.2 15.1 %collective-permute-start.4 = (f32[2,1,32,256]{3,2,1,0:T(8,128)S(1)}, f32[2,1,32,256]{3,2,1,0:T(8,128)S(1)}, u32[]{:S(2)}, u32[]{:S(2)}) collective-permute-start(f32[2,1,32,256]{3,2,1,0:T(8,128)S(1)} %get-tuple-element.89), channel_id=1, source_target_pairs={{0,128},{128,256},{256,384},{1,129},{129,257},{257,385},{2,130},{1... | collective-permute-start | bytes 196616 | tf_op jit(solution)/shard_map/ppermute | solution.py:18
  118.9 75.0 %collective-permute-start.14 = (f32[4,34,1]{2,1,0:T(8,128)S(1)}, f32[4,34,1]{2,1,0:T(8,128)S(1)}, u32[]{:S(2)}, u32[]{:S(2)}) collective-permute-start(f32[4,34,1]{2,1,0:T(8,128)S(1)} %get-tuple-element.57), channel_id=1, source_target_pairs={{1,0},{2,1},{3,2},{4,3},{5,4},{6,5},{7,6},{8,7},{9,8},{10,9},{11,1... | collective-permute-start | bytes 1640 | tf_op jit(solution)/shard_map/ppermute | solution.py:21
  122.4 71.5 %collective-permute-start.15 = (f32[4,34,1]{2,1,0:T(8,128)S(1)}, f32[4,34,1]{2,1,0:T(8,128)S(1)}, u32[]{:S(2)}, u32[]{:S(2)}) collective-permute-start(f32[4,34,1]{2,1,0:T(8,128)S(1)} %get-tuple-element.58), channel_id=1, source_target_pairs={{0,1},{1,2},{2,3},{3,4},{4,5},{5,6},{6,7},{7,8},{8,9},{9,10},{10,1... | collective-permute-start | bytes 1640 | tf_op jit(solution)/shard_map/ppermute | solution.py:18
  124.3 49.2 %collective-permute-start.6 = (f32[2,4,1,256]{3,2,1,0:T(1,128)S(1)}, f32[2,4,1,256]{3,2,1,0:T(1,128)S(1)}, u32[]{:S(2)}, u32[]{:S(2)}) collective-permute-start(f32[2,4,1,256]{3,2,1,0:T(1,128)S(1)} %get-tuple-element.25), channel_id=1, source_target_pairs={{0,16},{16,32},{32,48},{48,64},{64,80},{80,96},{96,112},{1,17},{17... | collective-permute-start | bytes 24584 | tf_op jit(solution)/shard_map/ppermute | solution.py:18
  131.2 42.4 %collective-permute-start.7 = (f32[2,4,1,256]{3,2,1,0:T(1,128)S(1)}, f32[2,4,1,256]{3,2,1,0:T(1,128)S(1)}, u32[]{:S(2)}, u32[]{:S(2)}) collective-permute-start(f32[2,4,1,256]{3,2,1,0:T(1,128)S(1)} %get-tuple-element.26), channel_id=1, source_target_pairs={{16,0},{32,16},{48,32},{64,48},{80,64},{96,80},{112,96},{17,1},{33... | collective-permute-start | bytes 24584 | tf_op jit(solution)/shard_map/ppermute | solution.py:21
  173.8 19.9 %collective-permute-start.8 = (f32[2,4,34,1]{3,2,1,0:T(8,128)S(1)}, f32[2,4,34,1]{3,2,1,0:T(8,128)S(1)}, u32[]{:S(2)}, u32[]{:S(2)}) collective-permute-start(f32[2,4,34,1]{3,2,1,0:T(8,128)S(1)} %get-tuple-element.23), channel_id=1, source_target_pairs={{0,1},{1,2},{2,3},{3,4},{4,5},{5,6},{6,7},{7,8},{8,9},{9,10},{10,1... | collective-permute-start | bytes 3272 | tf_op jit(solution)/shard_map/ppermute | solution.py:18
  175.7 18.0 %collective-permute-start.9 = (f32[2,4,34,1]{3,2,1,0:T(8,128)S(1)}, f32[2,4,34,1]{3,2,1,0:T(8,128)S(1)}, u32[]{:S(2)}, u32[]{:S(2)}) collective-permute-start(f32[2,4,34,1]{3,2,1,0:T(8,128)S(1)} %get-tuple-element.24), channel_id=1, source_target_pairs={{1,0},{2,1},{3,2},{4,3},{5,4},{6,5},{7,6},{8,7},{9,8},{10,9},{11,1... | collective-permute-start | bytes 3272 | tf_op jit(solution)/shard_map/ppermute | solution.py:21
  237.5 19.0 %collective-permute-start.24 = (f32[4,1,256]{2,1,0:T(1,128)S(1)}, f32[4,1,256]{2,1,0:T(1,128)S(1)}, u32[]{:S(2)}, u32[]{:S(2)}) collective-permute-start(f32[4,1,256]{2,1,0:T(1,128)S(1)} %get-tuple-element.85), channel_id=1, source_target_pairs={{0,16},{16,32},{32,48},{48,64},{64,80},{80,96},{96,112},{1,17},{17... | collective-permute-start | bytes 12296 | tf_op jit(solution)/shard_map/ppermute | solution.py:18
  239.4 17.1 %collective-permute-start.25 = (f32[4,1,256]{2,1,0:T(1,128)S(1)}, f32[4,1,256]{2,1,0:T(1,128)S(1)}, u32[]{:S(2)}, u32[]{:S(2)}) collective-permute-start(f32[4,1,256]{2,1,0:T(1,128)S(1)} %get-tuple-element.86), channel_id=1, source_target_pairs={{16,0},{32,16},{48,32},{64,48},{80,64},{96,80},{112,96},{17,1},{33... | collective-permute-start | bytes 12296 | tf_op jit(solution)/shard_map/ppermute | solution.py:21
  256.7 14.4 %collective-permute-start.26 = (f32[4,34,1]{2,1,0:T(8,128)S(1)}, f32[4,34,1]{2,1,0:T(8,128)S(1)}, u32[]{:S(2)}, u32[]{:S(2)}) collective-permute-start(f32[4,34,1]{2,1,0:T(8,128)S(1)} %get-tuple-element.53), channel_id=1, source_target_pairs={{1,0},{2,1},{3,2},{4,3},{5,4},{6,5},{7,6},{8,7},{9,8},{10,9},{11,1... | collective-permute-start | bytes 1640 | tf_op jit(solution)/shard_map/ppermute | solution.py:21
  258.6 12.5 %collective-permute-start.27 = (f32[4,34,1]{2,1,0:T(8,128)S(1)}, f32[4,34,1]{2,1,0:T(8,128)S(1)}, u32[]{:S(2)}, u32[]{:S(2)}) collective-permute-start(f32[4,34,1]{2,1,0:T(8,128)S(1)} %get-tuple-element.54), channel_id=1, source_target_pairs={{0,1},{1,2},{2,3},{3,4},{4,5},{5,6},{6,7},{7,8},{8,9},{9,10},{10,1... | collective-permute-start | bytes 1640 | tf_op jit(solution)/shard_map/ppermute | solution.py:18
  261.0 13.7 %collective-permute-start.66 = (f32[1,256]{1,0:T(1,128)S(1)}, f32[1,256]{1,0:T(1,128)S(1)}, u32[]{:S(2)}, u32[]{:S(2)}) collective-permute-start(f32[1,256]{1,0:T(1,128)S(1)} %get-tuple-element.157), channel_id=1, source_target_pairs={{0,16},{16,32},{32,48},{48,64},{64,80},{80,96},{96,112},{1,17},{17... | collective-permute-start | bytes 3080 | tf_op jit(solution)/shard_map/ppermute | solution.py:18
  280.5 17.4 %collective-permute-start.30 = (f32[4,1,256]{2,1,0:T(1,128)S(1)}, f32[4,1,256]{2,1,0:T(1,128)S(1)}, u32[]{:S(2)}, u32[]{:S(2)}) collective-permute-start(f32[4,1,256]{2,1,0:T(1,128)S(1)} %get-tuple-element.83), channel_id=1, source_target_pairs={{0,16},{16,32},{32,48},{48,64},{64,80},{80,96},{96,112},{1,17},{17... | collective-permute-start | bytes 12296 | tf_op jit(solution)/shard_map/ppermute | solution.py:18
  289.1 11.5 %collective-permute-start.31 = (f32[4,1,256]{2,1,0:T(1,128)S(1)}, f32[4,1,256]{2,1,0:T(1,128)S(1)}, u32[]{:S(2)}, u32[]{:S(2)}) collective-permute-start(f32[4,1,256]{2,1,0:T(1,128)S(1)} %get-tuple-element.84), channel_id=1, source_target_pairs={{16,0},{32,16},{48,32},{64,48},{80,64},{96,80},{112,96},{17,1},{33... | collective-permute-start | bytes 12296 | tf_op jit(solution)/shard_map/ppermute | solution.py:21
  291.1 14.0 %collective-permute-start.68 = (f32[34,1]{1,0:T(8,128)S(1)}, f32[34,1]{1,0:T(8,128)S(1)}, u32[]{:S(2)}, u32[]{:S(2)}) collective-permute-start(f32[34,1]{1,0:T(8,128)S(1)} %get-tuple-element.148), channel_id=1, source_target_pairs={{0,1},{1,2},{2,3},{3,4},{4,5},{5,6},{6,7},{7,8},{8,9},{9,10},{10,1... | collective-permute-start | bytes 416 | tf_op jit(solution)/shard_map/ppermute | solution.py:18
  293.1 12.1 %collective-permute-start.69 = (f32[34,1]{1,0:T(8,128)S(1)}, f32[34,1]{1,0:T(8,128)S(1)}, u32[]{:S(2)}, u32[]{:S(2)}) collective-permute-start(f32[34,1]{1,0:T(8,128)S(1)} %get-tuple-element.147), channel_id=1, source_target_pairs={{1,0},{2,1},{3,2},{4,3},{5,4},{6,5},{7,6},{8,7},{9,8},{10,9},{11,1... | collective-permute-start | bytes 416 | tf_op jit(solution)/shard_map/ppermute | solution.py:21
  309.8 23.4 %collective-permute-start.42 = (f32[1,32,256]{2,1,0:T(8,128)S(1)}, f32[1,32,256]{2,1,0:T(8,128)S(1)}, u32[]{:S(2)}, u32[]{:S(2)}) collective-permute-start(f32[1,32,256]{2,1,0:T(8,128)S(1)} %get-tuple-element.128), channel_id=1, source_target_pairs={{0,128},{128,256},{256,384},{1,129},{129,257},{257,385},{2,130},{1... | collective-permute-start | bytes 98312 | tf_op jit(solution)/shard_map/ppermute | solution.py:18
  312.7 20.5 %collective-permute-start.43 = (f32[1,32,256]{2,1,0:T(8,128)S(1)}, f32[1,32,256]{2,1,0:T(8,128)S(1)}, u32[]{:S(2)}, u32[]{:S(2)}) collective-permute-start(f32[1,32,256]{2,1,0:T(8,128)S(1)} %get-tuple-element.129), channel_id=1, source_target_pairs={{128,0},{256,128},{384,256},{129,1},{257,129},{385,257},{130,2},{2... | collective-permute-start | bytes 98312 | tf_op jit(solution)/shard_map/ppermute | solution.py:21
  340.4 11.5 %collective-permute-start.45 = (f32[4,1,256]{2,1,0:T(1,128)S(1)}, f32[4,1,256]{2,1,0:T(1,128)S(1)}, u32[]{:S(2)}, u32[]{:S(2)}) collective-permute-start(f32[4,1,256]{2,1,0:T(1,128)S(1)} %get-tuple-element.82), channel_id=1, source_target_pairs={{16,0},{32,16},{48,32},{64,48},{80,64},{96,80},{112,96},{17,1},{33... | collective-permute-start | bytes 12296 | tf_op jit(solution)/shard_map/ppermute | solution.py:21
  352.1 17.5 %collective-permute-start.46 = (f32[4,34,1]{2,1,0:T(8,128)S(1)}, f32[4,34,1]{2,1,0:T(8,128)S(1)}, u32[]{:S(2)}, u32[]{:S(2)}) collective-permute-start(f32[4,34,1]{2,1,0:T(8,128)S(1)} %get-tuple-element.49), channel_id=1, source_target_pairs={{1,0},{2,1},{3,2},{4,3},{5,4},{6,5},{7,6},{8,7},{9,8},{10,9},{11,1... | collective-permute-start | bytes 1640 | tf_op jit(solution)/shard_map/ppermute | solution.py:21
  354.0 15.6 %collective-permute-start.47 = (f32[4,34,1]{2,1,0:T(8,128)S(1)}, f32[4,34,1]{2,1,0:T(8,128)S(1)}, u32[]{:S(2)}, u32[]{:S(2)}) collective-permute-start(f32[4,34,1]{2,1,0:T(8,128)S(1)} %get-tuple-element.50), channel_id=1, source_target_pairs={{0,1},{1,2},{2,3},{3,4},{4,5},{5,6},{6,7},{7,8},{8,9},{9,10},{10,1... | collective-permute-start | bytes 1640 | tf_op jit(solution)/shard_map/ppermute | solution.py:18
  378.8 11.5 %collective-permute-start.51 = (f32[4,1,256]{2,1,0:T(1,128)S(1)}, f32[4,1,256]{2,1,0:T(1,128)S(1)}, u32[]{:S(2)}, u32[]{:S(2)}) collective-permute-start(f32[4,1,256]{2,1,0:T(1,128)S(1)} %get-tuple-element.80), channel_id=1, source_target_pairs={{16,0},{32,16},{48,32},{64,48},{80,64},{96,80},{112,96},{17,1},{33... | collective-permute-start | bytes 12296 | tf_op jit(solution)/shard_map/ppermute | solution.py:21
  408.9 19.0 %collective-permute-start.56 = (f32[4,1,256]{2,1,0:T(1,128)S(1)}, f32[4,1,256]{2,1,0:T(1,128)S(1)}, u32[]{:S(2)}, u32[]{:S(2)}) collective-permute-start(f32[4,1,256]{2,1,0:T(1,128)S(1)} %get-tuple-element.77), channel_id=1, source_target_pairs={{0,16},{16,32},{32,48},{48,64},{64,80},{80,96},{96,112},{1,17},{17... | collective-permute-start | bytes 12296 | tf_op jit(solution)/shard_map/ppermute | solution.py:18
  410.9 17.1 %collective-permute-start.57 = (f32[4,1,256]{2,1,0:T(1,128)S(1)}, f32[4,1,256]{2,1,0:T(1,128)S(1)}, u32[]{:S(2)}, u32[]{:S(2)}) collective-permute-start(f32[4,1,256]{2,1,0:T(1,128)S(1)} %get-tuple-element.78), channel_id=1, source_target_pairs={{16,0},{32,16},{48,32},{64,48},{80,64},{96,80},{112,96},{17,1},{33... | collective-permute-start | bytes 12296 | tf_op jit(solution)/shard_map/ppermute | solution.py:21
  428.1 14.2 %collective-permute-start.58 = (f32[4,34,1]{2,1,0:T(8,128)S(1)}, f32[4,34,1]{2,1,0:T(8,128)S(1)}, u32[]{:S(2)}, u32[]{:S(2)}) collective-permute-start(f32[4,34,1]{2,1,0:T(8,128)S(1)} %get-tuple-element.45), channel_id=1, source_target_pairs={{1,0},{2,1},{3,2},{4,3},{5,4},{6,5},{7,6},{8,7},{9,8},{10,9},{11,1... | collective-permute-start | bytes 1640 | tf_op jit(solution)/shard_map/ppermute | solution.py:21
  430.0 12.3 %collective-permute-start.59 = (f32[4,34,1]{2,1,0:T(8,128)S(1)}, f32[4,34,1]{2,1,0:T(8,128)S(1)}, u32[]{:S(2)}, u32[]{:S(2)}) collective-permute-start(f32[4,34,1]{2,1,0:T(8,128)S(1)} %get-tuple-element.46), channel_id=1, source_target_pairs={{0,1},{1,2},{2,3},{3,4},{4,5},{5,6},{6,7},{7,8},{8,9},{9,10},{10,1... | collective-permute-start | bytes 1640 | tf_op jit(solution)/shard_map/ppermute | solution.py:18
  432.4 12.6 %collective-permute-start.94 = (f32[1,256]{1,0:T(1,128)S(1)}, f32[1,256]{1,0:T(1,128)S(1)}, u32[]{:S(2)}, u32[]{:S(2)}) collective-permute-start(f32[1,256]{1,0:T(1,128)S(1)} %get-tuple-element.155), channel_id=1, source_target_pairs={{0,16},{16,32},{32,48},{48,64},{64,80},{80,96},{96,112},{1,17},{17... | collective-permute-start | bytes 3080 | tf_op jit(solution)/shard_map/ppermute | solution.py:18
  451.9 16.4 %collective-permute-start.62 = (f32[4,1,256]{2,1,0:T(1,128)S(1)}, f32[4,1,256]{2,1,0:T(1,128)S(1)}, u32[]{:S(2)}, u32[]{:S(2)}) collective-permute-start(f32[4,1,256]{2,1,0:T(1,128)S(1)} %get-tuple-element.75), channel_id=1, source_target_pairs={{0,16},{16,32},{32,48},{48,64},{64,80},{80,96},{96,112},{1,17},{17... | collective-permute-start | bytes 12296 | tf_op jit(solution)/shard_map/ppermute | solution.py:18
  459.5 11.5 %collective-permute-start.63 = (f32[4,1,256]{2,1,0:T(1,128)S(1)}, f32[4,1,256]{2,1,0:T(1,128)S(1)}, u32[]{:S(2)}, u32[]{:S(2)}) collective-permute-start(f32[4,1,256]{2,1,0:T(1,128)S(1)} %get-tuple-element.76), channel_id=1, source_target_pairs={{16,0},{32,16},{48,32},{64,48},{80,64},{96,80},{112,96},{17,1},{33... | collective-permute-start | bytes 12296 | tf_op jit(solution)/shard_map/ppermute | solution.py:21
  461.6 14.0 %collective-permute-start.96 = (f32[34,1]{1,0:T(8,128)S(1)}, f32[34,1]{1,0:T(8,128)S(1)}, u32[]{:S(2)}, u32[]{:S(2)}) collective-permute-start(f32[34,1]{1,0:T(8,128)S(1)} %get-tuple-element.146), channel_id=1, source_target_pairs={{0,1},{1,2},{2,3},{3,4},{4,5},{5,6},{6,7},{7,8},{8,9},{9,10},{10,1... | collective-permute-start | bytes 416 | tf_op jit(solution)/shard_map/ppermute | solution.py:18
  463.5 12.1 %collective-permute-start.97 = (f32[34,1]{1,0:T(8,128)S(1)}, f32[34,1]{1,0:T(8,128)S(1)}, u32[]{:S(2)}, u32[]{:S(2)}) collective-permute-start(f32[34,1]{1,0:T(8,128)S(1)} %get-tuple-element.145), channel_id=1, source_target_pairs={{1,0},{2,1},{3,2},{4,3},{5,4},{6,5},{7,6},{8,7},{9,8},{10,9},{11,1... | collective-permute-start | bytes 416 | tf_op jit(solution)/shard_map/ppermute | solution.py:21
  480.2 23.3 %collective-permute-start.70 = (f32[1,32,256]{2,1,0:T(8,128)S(1)}, f32[1,32,256]{2,1,0:T(8,128)S(1)}, u32[]{:S(2)}, u32[]{:S(2)}) collective-permute-start(f32[1,32,256]{2,1,0:T(8,128)S(1)} %get-tuple-element.119), channel_id=1, source_target_pairs={{0,128},{128,256},{256,384},{1,129},{129,257},{257,385},{2,130},{1... | collective-permute-start | bytes 98312 | tf_op jit(solution)/shard_map/ppermute | solution.py:18
  483.9 19.6 %collective-permute-start.71 = (f32[1,32,256]{2,1,0:T(8,128)S(1)}, f32[1,32,256]{2,1,0:T(8,128)S(1)}, u32[]{:S(2)}, u32[]{:S(2)}) collective-permute-start(f32[1,32,256]{2,1,0:T(8,128)S(1)} %get-tuple-element.120), channel_id=1, source_target_pairs={{128,0},{256,128},{384,256},{129,1},{257,129},{385,257},{130,2},{2... | collective-permute-start | bytes 98312 | tf_op jit(solution)/shard_map/ppermute | solution.py:21
  522.4 17.5 %collective-permute-start.74 = (f32[4,34,1]{2,1,0:T(8,128)S(1)}, f32[4,34,1]{2,1,0:T(8,128)S(1)}, u32[]{:S(2)}, u32[]{:S(2)}) collective-permute-start(f32[4,34,1]{2,1,0:T(8,128)S(1)} %get-tuple-element.41), channel_id=1, source_target_pairs={{1,0},{2,1},{3,2},{4,3},{5,4},{6,5},{7,6},{8,7},{9,8},{10,9},{11,1... | collective-permute-start | bytes 1640 | tf_op jit(solution)/shard_map/ppermute | solution.py:21
  524.4 15.6 %collective-permute-start.75 = (f32[4,34,1]{2,1,0:T(8,128)S(1)}, f32[4,34,1]{2,1,0:T(8,128)S(1)}, u32[]{:S(2)}, u32[]{:S(2)}) collective-permute-start(f32[4,34,1]{2,1,0:T(8,128)S(1)} %get-tuple-element.42), channel_id=1, source_target_pairs={{0,1},{1,2},{2,3},{3,4},{4,5},{5,6},{6,7},{7,8},{8,9},{9,10},{10,1... | collective-permute-start | bytes 1640 | tf_op jit(solution)/shard_map/ppermute | solution.py:18
  549.2 11.5 %collective-permute-start.79 = (f32[4,1,256]{2,1,0:T(1,128)S(1)}, f32[4,1,256]{2,1,0:T(1,128)S(1)}, u32[]{:S(2)}, u32[]{:S(2)}) collective-permute-start(f32[4,1,256]{2,1,0:T(1,128)S(1)} %get-tuple-element.72), channel_id=1, source_target_pairs={{16,0},{32,16},{48,32},{64,48},{80,64},{96,80},{112,96},{17,1},{33... | collective-permute-start | bytes 12296 | tf_op jit(solution)/shard_map/ppermute | solution.py:21
  579.3 19.0 %collective-permute-start.84 = (f32[4,1,256]{2,1,0:T(1,128)S(1)}, f32[4,1,256]{2,1,0:T(1,128)S(1)}, u32[]{:S(2)}, u32[]{:S(2)}) collective-permute-start(f32[4,1,256]{2,1,0:T(1,128)S(1)} %get-tuple-element.69), channel_id=1, source_target_pairs={{0,16},{16,32},{32,48},{48,64},{64,80},{80,96},{96,112},{1,17},{17... | collective-permute-start | bytes 12296 | tf_op jit(solution)/shard_map/ppermute | solution.py:18
  581.2 17.1 %collective-permute-start.85 = (f32[4,1,256]{2,1,0:T(1,128)S(1)}, f32[4,1,256]{2,1,0:T(1,128)S(1)}, u32[]{:S(2)}, u32[]{:S(2)}) collective-permute-start(f32[4,1,256]{2,1,0:T(1,128)S(1)} %get-tuple-element.70), channel_id=1, source_target_pairs={{16,0},{32,16},{48,32},{64,48},{80,64},{96,80},{112,96},{17,1},{33... | collective-permute-start | bytes 12296 | tf_op jit(solution)/shard_map/ppermute | solution.py:21
  598.5 14.2 %collective-permute-start.86 = (f32[4,34,1]{2,1,0:T(8,128)S(1)}, f32[4,34,1]{2,1,0:T(8,128)S(1)}, u32[]{:S(2)}, u32[]{:S(2)}) collective-permute-start(f32[4,34,1]{2,1,0:T(8,128)S(1)} %get-tuple-element.37), channel_id=1, source_target_pairs={{1,0},{2,1},{3,2},{4,3},{5,4},{6,5},{7,6},{8,7},{9,8},{10,9},{11,1... | collective-permute-start | bytes 1640 | tf_op jit(solution)/shard_map/ppermute | solution.py:21
  600.4 12.3 %collective-permute-start.87 = (f32[4,34,1]{2,1,0:T(8,128)S(1)}, f32[4,34,1]{2,1,0:T(8,128)S(1)}, u32[]{:S(2)}, u32[]{:S(2)}) collective-permute-start(f32[4,34,1]{2,1,0:T(8,128)S(1)} %get-tuple-element.38), channel_id=1, source_target_pairs={{0,1},{1,2},{2,3},{3,4},{4,5},{5,6},{6,7},{7,8},{8,9},{9,10},{10,1... | collective-permute-start | bytes 1640 | tf_op jit(solution)/shard_map/ppermute | solution.py:18
  602.8 12.6 %collective-permute-start.122 = (f32[1,256]{1,0:T(1,128)S(1)}, f32[1,256]{1,0:T(1,128)S(1)}, u32[]{:S(2)}, u32[]{:S(2)}) collective-permute-start(f32[1,256]{1,0:T(1,128)S(1)} %get-tuple-element.153), channel_id=1, source_target_pairs={{0,16},{16,32},{32,48},{48,64},{64,80},{80,96},{96,112},{1,17},{17... | collective-permute-start | bytes 3080 | tf_op jit(solution)/shard_map/ppermute | solution.py:18
  622.3 16.4 %collective-permute-start.90 = (f32[4,1,256]{2,1,0:T(1,128)S(1)}, f32[4,1,256]{2,1,0:T(1,128)S(1)}, u32[]{:S(2)}, u32[]{:S(2)}) collective-permute-start(f32[4,1,256]{2,1,0:T(1,128)S(1)} %get-tuple-element.67), channel_id=1, source_target_pairs={{0,16},{16,32},{32,48},{48,64},{64,80},{80,96},{96,112},{1,17},{17... | collective-permute-start | bytes 12296 | tf_op jit(solution)/shard_map/ppermute | solution.py:18
  629.9 11.5 %collective-permute-start.91 = (f32[4,1,256]{2,1,0:T(1,128)S(1)}, f32[4,1,256]{2,1,0:T(1,128)S(1)}, u32[]{:S(2)}, u32[]{:S(2)}) collective-permute-start(f32[4,1,256]{2,1,0:T(1,128)S(1)} %get-tuple-element.68), channel_id=1, source_target_pairs={{16,0},{32,16},{48,32},{64,48},{80,64},{96,80},{112,96},{17,1},{33... | collective-permute-start | bytes 12296 | tf_op jit(solution)/shard_map/ppermute | solution.py:21
  631.9 14.0 %collective-permute-start.124 = (f32[34,1]{1,0:T(8,128)S(1)}, f32[34,1]{1,0:T(8,128)S(1)}, u32[]{:S(2)}, u32[]{:S(2)}) collective-permute-start(f32[34,1]{1,0:T(8,128)S(1)} %get-tuple-element.144), channel_id=1, source_target_pairs={{0,1},{1,2},{2,3},{3,4},{4,5},{5,6},{6,7},{7,8},{8,9},{9,10},{10,1... | collective-permute-start | bytes 416 | tf_op jit(solution)/shard_map/ppermute | solution.py:18
  633.8 12.1 %collective-permute-start.125 = (f32[34,1]{1,0:T(8,128)S(1)}, f32[34,1]{1,0:T(8,128)S(1)}, u32[]{:S(2)}, u32[]{:S(2)}) collective-permute-start(f32[34,1]{1,0:T(8,128)S(1)} %get-tuple-element.143), channel_id=1, source_target_pairs={{1,0},{2,1},{3,2},{4,3},{5,4},{6,5},{7,6},{8,7},{9,8},{10,9},{11,1... | collective-permute-start | bytes 416 | tf_op jit(solution)/shard_map/ppermute | solution.py:21
  650.6 23.3 %collective-permute-start.98 = (f32[1,32,256]{2,1,0:T(8,128)S(1)}, f32[1,32,256]{2,1,0:T(8,128)S(1)}, u32[]{:S(2)}, u32[]{:S(2)}) collective-permute-start(f32[1,32,256]{2,1,0:T(8,128)S(1)} %get-tuple-element.110), channel_id=1, source_target_pairs={{0,128},{128,256},{256,384},{1,129},{129,257},{257,385},{2,130},{1... | collective-permute-start | bytes 98312 | tf_op jit(solution)/shard_map/ppermute | solution.py:18
  654.3 19.6 %collective-permute-start.99 = (f32[1,32,256]{2,1,0:T(8,128)S(1)}, f32[1,32,256]{2,1,0:T(8,128)S(1)}, u32[]{:S(2)}, u32[]{:S(2)}) collective-permute-start(f32[1,32,256]{2,1,0:T(8,128)S(1)} %get-tuple-element.111), channel_id=1, source_target_pairs={{128,0},{256,128},{384,256},{129,1},{257,129},{385,257},{130,2},{2... | collective-permute-start | bytes 98312 | tf_op jit(solution)/shard_map/ppermute | solution.py:21
  681.2 11.5 %collective-permute-start.101 = (f32[4,1,256]{2,1,0:T(1,128)S(1)}, f32[4,1,256]{2,1,0:T(1,128)S(1)}, u32[]{:S(2)}, u32[]{:S(2)}) collective-permute-start(f32[4,1,256]{2,1,0:T(1,128)S(1)} %get-tuple-element.66), channel_id=1, source_target_pairs={{16,0},{32,16},{48,32},{64,48},{80,64},{96,80},{112,96},{17,1},{33... | collective-permute-start | bytes 12296 | tf_op jit(solution)/shard_map/ppermute | solution.py:21
  692.8 17.5 %collective-permute-start.102 = (f32[4,34,1]{2,1,0:T(8,128)S(1)}, f32[4,34,1]{2,1,0:T(8,128)S(1)}, u32[]{:S(2)}, u32[]{:S(2)}) collective-permute-start(f32[4,34,1]{2,1,0:T(8,128)S(1)} %get-tuple-element.33), channel_id=1, source_target_pairs={{1,0},{2,1},{3,2},{4,3},{5,4},{6,5},{7,6},{8,7},{9,8},{10,9},{11,1... | collective-permute-start | bytes 1640 | tf_op jit(solution)/shard_map/ppermute | solution.py:21
  694.7 15.6 %collective-permute-start.103 = (f32[4,34,1]{2,1,0:T(8,128)S(1)}, f32[4,34,1]{2,1,0:T(8,128)S(1)}, u32[]{:S(2)}, u32[]{:S(2)}) collective-permute-start(f32[4,34,1]{2,1,0:T(8,128)S(1)} %get-tuple-element.34), channel_id=1, source_target_pairs={{0,1},{1,2},{2,3},{3,4},{4,5},{5,6},{6,7},{7,8},{8,9},{9,10},{10,1... | collective-permute-start | bytes 1640 | tf_op jit(solution)/shard_map/ppermute | solution.py:18
  751.6 11.5 %collective-permute-start.113 = (f32[4,1,256]{2,1,0:T(1,128)S(1)}, f32[4,1,256]{2,1,0:T(1,128)S(1)}, u32[]{:S(2)}, u32[]{:S(2)}) collective-permute-start(f32[4,1,256]{2,1,0:T(1,128)S(1)} %get-tuple-element.62), channel_id=1, source_target_pairs={{16,0},{32,16},{48,32},{64,48},{80,64},{96,80},{112,96},{17,1},{33... | collective-permute-start | bytes 12296 | tf_op jit(solution)/shard_map/ppermute | solution.py:21
  782.0 11.5 %collective-permute-start.119 = (f32[4,1,256]{2,1,0:T(1,128)S(1)}, f32[4,1,256]{2,1,0:T(1,128)S(1)}, u32[]{:S(2)}, u32[]{:S(2)}) collective-permute-start(f32[4,1,256]{2,1,0:T(1,128)S(1)} %get-tuple-element.60), channel_id=1, source_target_pairs={{16,0},{32,16},{48,32},{64,48},{80,64},{96,80},{112,96},{17,1},{33... | collective-permute-start | bytes 12296 | tf_op jit(solution)/shard_map/ppermute | solution.py:21
  793.6 17.5 %collective-permute-start.120 = (f32[4,34,1]{2,1,0:T(8,128)S(1)}, f32[4,34,1]{2,1,0:T(8,128)S(1)}, u32[]{:S(2)}, u32[]{:S(2)}) collective-permute-start(f32[4,34,1]{2,1,0:T(8,128)S(1)} %get-tuple-element.27), channel_id=1, source_target_pairs={{1,0},{2,1},{3,2},{4,3},{5,4},{6,5},{7,6},{8,7},{9,8},{10,9},{11,1... | collective-permute-start | bytes 1640 | tf_op jit(solution)/shard_map/ppermute | solution.py:21
  795.5 15.6 %collective-permute-start.121 = (f32[4,34,1]{2,1,0:T(8,128)S(1)}, f32[4,34,1]{2,1,0:T(8,128)S(1)}, u32[]{:S(2)}, u32[]{:S(2)}) collective-permute-start(f32[4,34,1]{2,1,0:T(8,128)S(1)} %get-tuple-element.28), channel_id=1, source_target_pairs={{0,1},{1,2},{2,3},{3,4},{4,5},{5,6},{6,7},{7,8},{8,9},{9,10},{10,1... | collective-permute-start | bytes 1640 | tf_op jit(solution)/shard_map/ppermute | solution.py:18
  (71 other events, 766.8 us)
Sparse Core Ops, SparseCore 0:
  115.2 56.7 all-reduce.2
where the time goes:
time: 824 us; the launch traced here: 819 us
  starting transfers between devices  379 us (46%)
  waiting for transfers between devices  229 us (28%)
  blocking collectives  161 us (20%)
  between operations  16.3 us (2%)
  local copies, waits for them, and re-layouts  13.5 us (2%)
  other arithmetic  11.3 us (1%)
  matrix products  9.98 us (1%)
    ppermute x63, starting transfers between devices, padded(): lax.ppermute(lax.slice_in_dim(block, block.shape[dim] - width, None, axis...  234 us
    ppermute x63, waiting for transfers between devices, padded(): lax.ppermute(lax.slice_in_dim(block, 0, width, axis=dim), axis, backward)  151 us
    ppermute x63, starting transfers between devices, padded(): lax.ppermute(lax.slice_in_dim(block, 0, width, axis=dim), axis, backward)  145 us
    psum x3, blocking collectives, spread(): return lax.psum(jnp.where(mine, value, jnp.zeros_like(value)), axis)  55.9 us
    all_gather x4, blocking collectives, shards(): lax.all_gather(source_strip, 'sec', axis=0, tiled=True)  52.7 us
    all_gather x4, blocking collectives, shards(): lax.all_gather(new_strip, 'sec', axis=0, tiled=True)  52.6 us
    psum x1, waiting for transfers between devices, spread(): return lax.psum(jnp.where(mine, value, jnp.zeros_like(value)), axis)  38.9 us
    ppermute x63, waiting for transfers between devices, padded(): lax.ppermute(lax.slice_in_dim(block, block.shape[dim] - width, None, axis...  38.6 us
  transfers between devices with their start and end apart: 127, of which 46 were waited for; matrix products, arithmetic and copies ran while one was open for 4% of the time, Pallas kernels for 0%

commit v1 on v0

--- a/solution.py
+++ b/solution.py
@@ -25,7 +25,7 @@
 
 def spread(value, axis, root):
     mine = lax.axis_index(axis) == root
-    return lax.psum(jnp.where(mine, value, jnp.zeros_like(value)), axis)
+    return jnp.sum(lax.all_gather(jnp.where(mine, value, jnp.zeros_like(value)), axis), axis=0)
 
 
 def infiltration(land_frac, top_cond, surface, top_press):

time: 824 us -> 810 us (0.983)
  waiting for transfers between devices: 229 us -> 195 us
  blocking collectives: 161 us -> 178 us
  between operations: 16.3 us -> 3.1 us
  other arithmetic: 11.3 us -> 22.1 us
    all_gather x0 -> x5, blocking collectives: none -> 71.8 us  [spread(): lax.all_gather(jnp.where(mine, value, jnp.zeros_like(value)), axis)]
    psum x3 -> x0, blocking collectives: 55.9 us -> none  [spread(): return lax.psum(jnp.where(mine, value, jnp.zeros_like(value)), axis)]
    psum x1 -> x0, waiting for transfers between devices: 38.9 us -> none  [spread(): return lax.psum(jnp.where(mine, value, jnp.zeros_like(value)), axis)]
    div x16, other arithmetic: 2.83 us -> 11.3 us  [jacobi_sweep(): return total / diagonal]
  transfers between devices with their start and end apart: 127 -> 126, of which waited for: 46 -> 45; matrix products, arithmetic and copies ran while one was open for 4% -> 4% of each run, Pallas kernels for 0% -> 0%
where the time goes in v1:
time: 810 us; the launch traced here: 806 us
  starting transfers between devices  380 us (47%)
  waiting for transfers between devices  195 us (24%)
  blocking collectives  178 us (22%)
  other arithmetic  22.1 us (3%)
  local copies, waits for them, and re-layouts  18.1 us (2%)
  matrix products  9.32 us (1%)
    ppermute x63, starting transfers between devices, padded(): lax.ppermute(lax.slice_in_dim(block, block.shape[dim] - width, None, axis...  234 us
    ppermute x63, waiting for transfers between devices, padded(): lax.ppermute(lax.slice_in_dim(block, 0, width, axis=dim), axis, backward)  154 us
    ppermute x63, starting transfers between devices, padded(): lax.ppermute(lax.slice_in_dim(block, 0, width, axis=dim), axis, backward)  146 us
    all_gather x5, blocking collectives, spread(): lax.all_gather(jnp.where(mine, value, jnp.zeros_like(value)), axis)  71.8 us
    all_gather x4, blocking collectives, shards(): lax.all_gather(source_strip, 'sec', axis=0, tiled=True)  53.8 us
    all_gather x4, blocking collectives, shards(): lax.all_gather(new_strip, 'sec', axis=0, tiled=True)  52.6 us
    ppermute x63, waiting for transfers between devices, padded(): lax.ppermute(lax.slice_in_dim(block, block.shape[dim] - width, None, axis...  41.3 us
  transfers between devices with their start and end apart: 126, of which 45 were waited for; matrix products, arithmetic and copies ran while one was open for 4% of the time, Pallas kernels for 0%

profile of v1, /device:TPU:38, one launch (start us, length us, event | category | flops | bytes accessed | tf_op | source)
XLA Modules:
  0.0 806.0 jit_solution(17257284937519495224)
XLA Ops:
  1.5 10.8 %collective-permute-start = (s32[2,1,256]{2,1,0:T(1,128)S(1)}, s32[2,1,256]{2,1,0:T(1,128)S(1)}, u32[]{:S(2)}, u32[]{:S(2)}) collective-permute-start(s32[2,1,256]{2,1,0:T(1,128)S(1)} %get-tuple-element.145), channel_id=1, source_target_pairs={{0,16},{16,32},{32,48},{48,64},{64,80},{80,96},{96,112},{1,17},{17... | collective-permute-start | bytes 6152 | tf_op jit(solution)/shard_map/ppermute | solution.py:18
  15.1 9.9 %collective-permute-start.38 = (f32[1,256]{1,0:T(1,128)S(1)}, f32[1,256]{1,0:T(1,128)S(1)}, u32[]{:S(2)}, u32[]{:S(2)}) collective-permute-start(f32[1,256]{1,0:T(1,128)S(1)} %get-tuple-element.165), channel_id=1, source_target_pairs={{0,16},{16,32},{32,48},{48,64},{64,80},{80,96},{96,112},{1,17},{17... | collective-permute-start | bytes 3080 | tf_op jit(solution)/shard_map/ppermute | solution.py:18
  27.7 9.9 %collective-permute-start.34 = (f32[1,256]{1,0:T(1,128)S(1)}, f32[1,256]{1,0:T(1,128)S(1)}, u32[]{:S(2)}, u32[]{:S(2)}) collective-permute-start(f32[1,256]{1,0:T(1,128)S(1)} %get-tuple-element.163), channel_id=1, source_target_pairs={{0,16},{16,32},{32,48},{48,64},{64,80},{80,96},{96,112},{1,17},{17... | collective-permute-start | bytes 3080 | tf_op jit(solution)/shard_map/ppermute | solution.py:18
  39.3 13.4 %all_gather.45 = f32[4,32,256]{2,1,0:T(8,128)S(1)} all-gather(f32[1,32,256]{2,1,0:T(8,128)S(1)} %copy.57), channel_id=1, replica_groups=mesh['sec'=4,'gx'=8,'gy'=16] {'sec'}, dimensions={0}, use_global_device_ids=true | all-gather | bytes 163840 | tf_op jit(solution)/shard_map/all_gather | solution.py:28
  62.2 6.2 collective-permute-done.35
  76.6 4.6 collective-permute-start.37
  83.3 4.9 collective-permute-start.3
  98.6 5.4 maximum_convert_fusion
  110.4 13.4 %all_gather.44 = f32[4,32,256]{2,1,0:T(8,128)S(1)} all-gather(f32[1,32,256]{2,1,0:T(8,128)S(1)} %copy.55), channel_id=1, replica_groups=mesh['sec'=4,'gx'=8,'gy'=16] {'sec'}, dimensions={0}, use_global_device_ids=true | all-gather | bytes 163840 | tf_op jit(solution)/shard_map/all_gather | solution.py:28
  127.6 14.4 %all_gather.46 = f32[32,256]{1,0:T(8,128)S(1)} all-gather(f32[8,256]{1,0:T(8,128)S(1)} %get-tuple-element.28), channel_id=1, replica_groups=mesh['sec'=4,'gx'=8,'gy'=16] {'sec'}, dimensions={0}, use_global_device_ids=true | all-gather | bytes 40960 | tf_op jit(solution)/shard_map/all_gather | solution.py:166
  142.1 7.8 collective-permute-start.12
  151.8 9.9 %collective-permute-start.6 = (f32[2,4,1,256]{3,1,2,0:T(4,128)S(1)}, f32[2,4,1,256]{3,1,2,0:T(4,128)S(1)}, u32[]{:S(2)}, u32[]{:S(2)}) collective-permute-start(f32[2,4,1,256]{3,1,2,0:T(4,128)S(1)} %get-tuple-element.32), channel_id=1, source_target_pairs={{0,16},{16,32},{32,48},{48,64},{64,80},{80,96},{96,112},{1,17},{17... | collective-permute-start | bytes 24584 | tf_op jit(solution)/shard_map/ppermute | solution.py:18
  163.8 9.5 %collective-permute-done.7 = f32[2,4,1,256]{3,1,2,0:T(4,128)S(1)} collective-permute-done((f32[2,4,1,256]{3,1,2,0:T(4,128)S(1)}, f32[2,4,1,256]{3,1,2,0:T(4,128)S(1)}, u32[]{:S(2)}, u32[]{:S(2)}) %collective-permute-start.7) | collective-permute-done | bytes 8224 | tf_op jit(solution)/shard_map/ppermute | solution.py:21
  175.6 4.9 collective-permute-start.9
  196.7 4.2 collective-permute-done.17
  206.8 7.6 collective-permute-done.19
  218.9 4.4 collective-permute-done.21
  228.5 4.2 collective-permute-done.23
  238.6 13.1 %all_gather.47 = f32[32,256]{1,0:T(8,128)S(1)} all-gather(f32[8,256]{1,0:T(8,128)S(1)} %get-tuple-element.14), channel_id=1, replica_groups=mesh['sec'=4,'gx'=8,'gy'=16] {'sec'}, dimensions={0}, use_global_device_ids=true | all-gather | bytes 40960 | tf_op jit(solution)/shard_map/all_gather | solution.py:165
  256.3 7.9 collective-permute-start.66
  270.3 5.4 collective-permute-done.67
  275.8 9.0 %collective-permute-start.30 = (f32[4,1,256]{2,0,1:T(4,128)S(1)}, f32[4,1,256]{2,0,1:T(4,128)S(1)}, u32[]{:S(2)}, u32[]{:S(2)}) collective-permute-start(f32[4,1,256]{2,0,1:T(4,128)S(1)} %get-tuple-element.90), channel_id=1, source_target_pairs={{0,16},{16,32},{32,48},{48,64},{64,80},{80,96},{96,112},{1,17},{17... | collective-permute-start | bytes 12296 | tf_op jit(solution)/shard_map/ppermute | solution.py:18
  288.7 4.9 collective-permute-start.69
  300.9 4.3 collective-permute-done.33
  310.1 15.2 %all_gather.48 = f32[4,32,256]{2,1,0:T(8,128)S(1)} all-gather(f32[1,32,256]{2,1,0:T(8,128)S(1)} %copy.65), channel_id=1, replica_groups=mesh['sec'=4,'gx'=8,'gy'=16] {'sec'}, dimensions={0}, use_global_device_ids=true | all-gather | bytes 163840 | tf_op jit(solution)/shard_map/all_gather | solution.py:28
  325.3 7.1 collective-permute-start.44
  334.5 9.5 %collective-permute-done.45 = f32[4,1,256]{2,0,1:T(4,128)S(1)} collective-permute-done((f32[4,1,256]{2,0,1:T(4,128)S(1)}, f32[4,1,256]{2,0,1:T(4,128)S(1)}, u32[]{:S(2)}, u32[]{:S(2)}) %collective-permute-start.45) | collective-permute-done | bytes 4128 | tf_op jit(solution)/shard_map/ppermute | solution.py:21
  348.5 13.1 %all_gather.49 = f32[32,256]{1,0:T(8,128)S(1)} all-gather(f32[8,256]{1,0:T(8,128)S(1)} %get-tuple-element.109), channel_id=1, replica_groups=mesh['sec'=4,'gx'=8,'gy'=16] {'sec'}, dimensions={0}, use_global_device_ids=true | all-gather | bytes 40960 | tf_op jit(solution)/shard_map/all_gather | solution.py:166
  365.9 4.3 collective-permute-done.49
  376.0 7.6 collective-permute-done.51
  388.2 4.4 collective-permute-done.53
  397.8 4.2 collective-permute-done.55
  407.9 13.1 %all_gather.50 = f32[32,256]{1,0:T(8,128)S(1)} all-gather(f32[8,256]{1,0:T(8,128)S(1)} %get-tuple-element.108), channel_id=1, replica_groups=mesh['sec'=4,'gx'=8,'gy'=16] {'sec'}, dimensions={0}, use_global_device_ids=true | all-gather | bytes 40960 | tf_op jit(solution)/shard_map/all_gather | solution.py:165
  425.6 7.9 collective-permute-start.94
  439.4 5.6 collective-permute-done.95
  445.1 8.8 %collective-permute-start.62 = (f32[4,1,256]{2,0,1:T(4,128)S(1)}, f32[4,1,256]{2,0,1:T(4,128)S(1)}, u32[]{:S(2)}, u32[]{:S(2)}) collective-permute-start(f32[4,1,256]{2,0,1:T(4,128)S(1)} %get-tuple-element.82), channel_id=1, source_target_pairs={{0,16},{16,32},{32,48},{48,64},{64,80},{80,96},{96,112},{1,17},{17... | collective-permute-start | bytes 12296 | tf_op jit(solution)/shard_map/ppermute | solution.py:18
  457.8 4.9 collective-permute-start.97
  470.1 4.3 collective-permute-done.65
  479.5 14.9 %all_gather.51 = f32[4,32,256]{2,1,0:T(8,128)S(1)} all-gather(f32[1,32,256]{2,1,0:T(8,128)S(1)} %copy.67), channel_id=1, replica_groups=mesh['sec'=4,'gx'=8,'gy'=16] {'sec'}, dimensions={0}, use_global_device_ids=true | all-gather | bytes 163840 | tf_op jit(solution)/shard_map/all_gather | solution.py:28
  494.5 7.1 collective-permute-start.72
  503.8 9.3 %collective-permute-done.73 = f32[4,1,256]{2,0,1:T(4,128)S(1)} collective-permute-done((f32[4,1,256]{2,0,1:T(4,128)S(1)}, f32[4,1,256]{2,0,1:T(4,128)S(1)}, u32[]{:S(2)}, u32[]{:S(2)}) %collective-permute-start.73) | collective-permute-done | bytes 4128 | tf_op jit(solution)/shard_map/ppermute | solution.py:21
  517.6 13.1 %all_gather.52 = f32[32,256]{1,0:T(8,128)S(1)} all-gather(f32[8,256]{1,0:T(8,128)S(1)} %get-tuple-element.107), channel_id=1, replica_groups=mesh['sec'=4,'gx'=8,'gy'=16] {'sec'}, dimensions={0}, use_global_device_ids=true | all-gather | bytes 40960 | tf_op jit(solution)/shard_map/all_gather | solution.py:166
  535.0 4.3 collective-permute-done.77
  545.2 7.6 collective-permute-done.79
  557.3 4.4 collective-permute-done.81
  566.9 4.2 collective-permute-done.83
  577.0 13.1 %all_gather.53 = f32[32,256]{1,0:T(8,128)S(1)} all-gather(f32[8,256]{1,0:T(8,128)S(1)} %get-tuple-element.106), channel_id=1, replica_groups=mesh['sec'=4,'gx'=8,'gy'=16] {'sec'}, dimensions={0}, use_global_device_ids=true | all-gather | bytes 40960 | tf_op jit(solution)/shard_map/all_gather | solution.py:165
  594.8 7.9 collective-permute-start.122
  608.6 5.6 collective-permute-done.123
  614.3 8.8 %collective-permute-start.90 = (f32[4,1,256]{2,0,1:T(4,128)S(1)}, f32[4,1,256]{2,0,1:T(4,128)S(1)}, u32[]{:S(2)}, u32[]{:S(2)}) collective-permute-start(f32[4,1,256]{2,0,1:T(4,128)S(1)} %get-tuple-element.74), channel_id=1, source_target_pairs={{0,16},{16,32},{32,48},{48,64},{64,80},{80,96},{96,112},{1,17},{17... | collective-permute-start | bytes 12296 | tf_op jit(solution)/shard_map/ppermute | solution.py:18
  627.0 4.9 collective-permute-start.125
  639.2 4.3 collective-permute-done.93
  648.6 14.9 %all_gather.54 = f32[4,32,256]{2,1,0:T(8,128)S(1)} all-gather(f32[1,32,256]{2,1,0:T(8,128)S(1)} %copy.69), channel_id=1, replica_groups=mesh['sec'=4,'gx'=8,'gy'=16] {'sec'}, dimensions={0}, use_global_device_ids=true | all-gather | bytes 163840 | tf_op jit(solution)/shard_map/all_gather | solution.py:28
  663.6 7.1 collective-permute-start.100
  672.7 9.5 %collective-permute-done.101 = f32[4,1,256]{2,0,1:T(4,128)S(1)} collective-permute-done((f32[4,1,256]{2,0,1:T(4,128)S(1)}, f32[4,1,256]{2,0,1:T(4,128)S(1)}, u32[]{:S(2)}, u32[]{:S(2)}) %collective-permute-start.101) | collective-permute-done | bytes 4128 | tf_op jit(solution)/shard_map/ppermute | solution.py:21
  686.8 13.1 %all_gather.55 = f32[32,256]{1,0:T(8,128)S(1)} all-gather(f32[8,256]{1,0:T(8,128)S(1)} %get-tuple-element.105), channel_id=1, replica_groups=mesh['sec'=4,'gx'=8,'gy'=16] {'sec'}, dimensions={0}, use_global_device_ids=true | all-gather | bytes 40960 | tf_op jit(solution)/shard_map/all_gather | solution.py:166
  704.1 4.3 collective-permute-done.105
  714.3 7.6 collective-permute-done.107
  726.4 4.4 collective-permute-done.109
  746.2 7.6 collective-permute-done.113
  758.3 4.4 collective-permute-done.115
  768.7 4.2 collective-permute-done.117
  778.8 7.6 collective-permute-done.119
  790.9 13.2 %all_gather.56 = f32[32,256]{1,0:T(8,128)S(1)} all-gather(f32[8,256]{1,0:T(8,128)S(1)} %get-tuple-element.104), channel_id=1, replica_groups=mesh['sec'=4,'gx'=8,'gy'=16] {'sec'}, dimensions={0}, use_global_device_ids=true | all-gather | bytes 40960 | tf_op jit(solution)/shard_map/all_gather | solution.py:165
  (384 shorter events, 295.3 us)
Async XLA Ops:
  1.5 75.1 %collective-permute-start = (s32[2,1,256]{2,1,0:T(1,128)S(1)}, s32[2,1,256]{2,1,0:T(1,128)S(1)}, u32[]{:S(2)}, u32[]{:S(2)}) collective-permute-start(s32[2,1,256]{2,1,0:T(1,128)S(1)} %get-tuple-element.145), channel_id=1, source_target_pairs={{0,16},{16,32},{32,48},{48,64},{64,80},{80,96},{96,112},{1,17},{17... | collective-permute-start | bytes 6152 | tf_op jit(solution)/shard_map/ppermute | solution.py:18
  12.3 68.9 %collective-permute-start.1 = (s32[2,1,256]{2,1,0:T(1,128)S(1)}, s32[2,1,256]{2,1,0:T(1,128)S(1)}, u32[]{:S(2)}, u32[]{:S(2)}) collective-permute-start(s32[2,1,256]{2,1,0:T(1,128)S(1)} %get-tuple-element.146), channel_id=1, source_target_pairs={{16,0},{32,16},{48,32},{64,48},{80,64},{96,80},{112,96},{17,1},{33... | collective-permute-start | bytes 6152 | tf_op jit(solution)/shard_map/ppermute | solution.py:21
  15.1 41.9 %collective-permute-start.38 = (f32[1,256]{1,0:T(1,128)S(1)}, f32[1,256]{1,0:T(1,128)S(1)}, u32[]{:S(2)}, u32[]{:S(2)}) collective-permute-start(f32[1,256]{1,0:T(1,128)S(1)} %get-tuple-element.165), channel_id=1, source_target_pairs={{0,16},{16,32},{32,48},{48,64},{64,80},{80,96},{96,112},{1,17},{17... | collective-permute-start | bytes 3080 | tf_op jit(solution)/shard_map/ppermute | solution.py:18
  25.0 33.8 %collective-permute-start.39 = (f32[1,256]{1,0:T(1,128)S(1)}, f32[1,256]{1,0:T(1,128)S(1)}, u32[]{:S(2)}, u32[]{:S(2)}) collective-permute-start(f32[1,256]{1,0:T(1,128)S(1)} %get-tuple-element.166), channel_id=1, source_target_pairs={{16,0},{32,16},{48,32},{64,48},{80,64},{96,80},{112,96},{17,1},{33... | collective-permute-start | bytes 3080 | tf_op jit(solution)/shard_map/ppermute | solution.py:21
  27.7 32.5 %collective-permute-start.34 = (f32[1,256]{1,0:T(1,128)S(1)}, f32[1,256]{1,0:T(1,128)S(1)}, u32[]{:S(2)}, u32[]{:S(2)}) collective-permute-start(f32[1,256]{1,0:T(1,128)S(1)} %get-tuple-element.163), channel_id=1, source_target_pairs={{0,16},{16,32},{32,48},{48,64},{64,80},{80,96},{96,112},{1,17},{17... | collective-permute-start | bytes 3080 | tf_op jit(solution)/shard_map/ppermute | solution.py:18
  58.8 83.2 %collective-permute-start.11 = (f32[1,32,256]{2,0,1:T(1,128)}, f32[1,32,256]{2,0,1:T(1,128)S(1)}, u32[]{:S(2)}, u32[]{:S(2)}) collective-permute-start(f32[1,32,256]{2,0,1:T(1,128)} %get-tuple-element.144), channel_id=1, source_target_pairs={{128,0},{256,128},{384,256},{129,1},{257,129},{385,257},{130,2},{2... | collective-permute-start | bytes 98312 | tf_op jit(solution)/shard_map/ppermute | solution.py:21
  70.4 71.6 %collective-permute-start.10 = (f32[1,32,256]{2,0,1:T(1,128)}, f32[1,32,256]{2,0,1:T(1,128)S(1)}, u32[]{:S(2)}, u32[]{:S(2)}) collective-permute-start(f32[1,32,256]{2,0,1:T(1,128)} %copy.59), channel_id=1, source_target_pairs={{0,128},{128,256},{256,384},{1,129},{129,257},{257,385},{2,130},{1... | collective-permute-start | bytes 98312 | tf_op jit(solution)/shard_map/ppermute | solution.py:18
  76.6 11.5 %collective-permute-start.37 = (f32[34,1]{1,0:T(8,128)S(1)}, f32[34,1]{1,0:T(8,128)S(1)}, u32[]{:S(2)}, u32[]{:S(2)}) collective-permute-start(f32[34,1]{1,0:T(8,128)S(1)} %get-tuple-element.153), channel_id=1, source_target_pairs={{1,0},{2,1},{3,2},{4,3},{5,4},{6,5},{7,6},{8,7},{9,8},{10,9},{11,1... | collective-permute-start | bytes 416 | tf_op jit(solution)/shard_map/ppermute | solution.py:21
  123.9 27.9 %collective-permute-start.4 = (f32[2,1,32,256]{3,1,2,0:T(1,128)S(1)}, f32[2,1,32,256]{3,1,2,0:T(1,128)S(1)}, u32[]{:S(2)}, u32[]{:S(2)}) collective-permute-start(f32[2,1,32,256]{3,1,2,0:T(1,128)S(1)} %get-tuple-element.96), channel_id=1, source_target_pairs={{0,128},{128,256},{256,384},{1,129},{129,257},{257,385},{2,130},{1... | collective-permute-start | bytes 196616 | tf_op jit(solution)/shard_map/ppermute | solution.py:18
  125.4 26.4 %collective-permute-start.5 = (f32[2,1,32,256]{3,1,2,0:T(1,128)S(1)}, f32[2,1,32,256]{3,1,2,0:T(1,128)S(1)}, u32[]{:S(2)}, u32[]{:S(2)}) collective-permute-start(f32[2,1,32,256]{3,1,2,0:T(1,128)S(1)} %get-tuple-element.97), channel_id=1, source_target_pairs={{128,0},{256,128},{384,256},{129,1},{257,129},{385,257},{130,2},{2... | collective-permute-start | bytes 196616 | tf_op jit(solution)/shard_map/ppermute | solution.py:21
  142.1 21.6 %collective-permute-start.12 = (f32[4,1,256]{2,0,1:T(4,128)S(1)}, f32[4,1,256]{2,0,1:T(4,128)S(1)}, u32[]{:S(2)}, u32[]{:S(2)}) collective-permute-start(f32[4,1,256]{2,0,1:T(4,128)S(1)} %get-tuple-element.98), channel_id=1, source_target_pairs={{0,16},{16,32},{32,48},{48,64},{64,80},{80,96},{96,112},{1,17},{17... | collective-permute-start | bytes 12296 | tf_op jit(solution)/shard_map/ppermute | solution.py:18
  149.8 13.9 %collective-permute-start.13 = (f32[4,1,256]{2,0,1:T(4,128)S(1)}, f32[4,1,256]{2,0,1:T(4,128)S(1)}, u32[]{:S(2)}, u32[]{:S(2)}) collective-permute-start(f32[4,1,256]{2,0,1:T(4,128)S(1)} %get-tuple-element.99), channel_id=1, source_target_pairs={{16,0},{32,16},{48,32},{64,48},{80,64},{96,80},{112,96},{17,1},{33... | collective-permute-start | bytes 12296 | tf_op jit(solution)/shard_map/ppermute | solution.py:21
  151.8 12.0 %collective-permute-start.6 = (f32[2,4,1,256]{3,1,2,0:T(4,128)S(1)}, f32[2,4,1,256]{3,1,2,0:T(4,128)S(1)}, u32[]{:S(2)}, u32[]{:S(2)}) collective-permute-start(f32[2,4,1,256]{3,1,2,0:T(4,128)S(1)} %get-tuple-element.32), channel_id=1, source_target_pairs={{0,16},{16,32},{32,48},{48,64},{64,80},{80,96},{96,112},{1,17},{17... | collective-permute-start | bytes 24584 | tf_op jit(solution)/shard_map/ppermute | solution.py:18
  161.8 11.6 %collective-permute-start.7 = (f32[2,4,1,256]{3,1,2,0:T(4,128)S(1)}, f32[2,4,1,256]{3,1,2,0:T(4,128)S(1)}, u32[]{:S(2)}, u32[]{:S(2)}) collective-permute-start(f32[2,4,1,256]{3,1,2,0:T(4,128)S(1)} %get-tuple-element.33), channel_id=1, source_target_pairs={{16,0},{32,16},{48,32},{64,48},{80,64},{96,80},{112,96},{17,1},{33... | collective-permute-start | bytes 24584 | tf_op jit(solution)/shard_map/ppermute | solution.py:21
  202.9 11.5 %collective-permute-start.19 = (f32[4,1,256]{2,0,1:T(4,128)S(1)}, f32[4,1,256]{2,0,1:T(4,128)S(1)}, u32[]{:S(2)}, u32[]{:S(2)}) collective-permute-start(f32[4,1,256]{2,0,1:T(4,128)S(1)} %get-tuple-element.95), channel_id=1, source_target_pairs={{16,0},{32,16},{48,32},{64,48},{80,64},{96,80},{112,96},{17,1},{33... | collective-permute-start | bytes 12296 | tf_op jit(solution)/shard_map/ppermute | solution.py:21
  232.7 19.0 %collective-permute-start.24 = (f32[4,1,256]{2,0,1:T(4,128)S(1)}, f32[4,1,256]{2,0,1:T(4,128)S(1)}, u32[]{:S(2)}, u32[]{:S(2)}) collective-permute-start(f32[4,1,256]{2,0,1:T(4,128)S(1)} %get-tuple-element.92), channel_id=1, source_target_pairs={{0,16},{16,32},{32,48},{48,64},{64,80},{80,96},{96,112},{1,17},{17... | collective-permute-start | bytes 12296 | tf_op jit(solution)/shard_map/ppermute | solution.py:18
  234.6 17.1 %collective-permute-start.25 = (f32[4,1,256]{2,0,1:T(4,128)S(1)}, f32[4,1,256]{2,0,1:T(4,128)S(1)}, u32[]{:S(2)}, u32[]{:S(2)}) collective-permute-start(f32[4,1,256]{2,0,1:T(4,128)S(1)} %get-tuple-element.93), channel_id=1, source_target_pairs={{16,0},{32,16},{48,32},{64,48},{80,64},{96,80},{112,96},{17,1},{33... | collective-permute-start | bytes 12296 | tf_op jit(solution)/shard_map/ppermute | solution.py:21
  251.9 14.2 %collective-permute-start.26 = (f32[4,34,1]{2,0,1:T(4,128)S(1)}, f32[4,34,1]{2,0,1:T(4,128)S(1)}, u32[]{:S(2)}, u32[]{:S(2)}) collective-permute-start(f32[4,34,1]{2,0,1:T(4,128)S(1)} %get-tuple-element.60), channel_id=1, source_target_pairs={{1,0},{2,1},{3,2},{4,3},{5,4},{6,5},{7,6},{8,7},{9,8},{10,9},{11,1... | collective-permute-start | bytes 1640 | tf_op jit(solution)/shard_map/ppermute | solution.py:21
  253.9 12.3 %collective-permute-start.27 = (f32[4,34,1]{2,0,1:T(4,128)S(1)}, f32[4,34,1]{2,0,1:T(4,128)S(1)}, u32[]{:S(2)}, u32[]{:S(2)}) collective-permute-start(f32[4,34,1]{2,0,1:T(4,128)S(1)} %get-tuple-element.61), channel_id=1, source_target_pairs={{0,1},{1,2},{2,3},{3,4},{4,5},{5,6},{6,7},{7,8},{8,9},{9,10},{10,1... | collective-permute-start | bytes 1640 | tf_op jit(solution)/shard_map/ppermute | solution.py:18
  256.3 14.0 %collective-permute-start.66 = (f32[1,256]{1,0:T(1,128)S(1)}, f32[1,256]{1,0:T(1,128)S(1)}, u32[]{:S(2)}, u32[]{:S(2)}) collective-permute-start(f32[1,256]{1,0:T(1,128)S(1)} %get-tuple-element.161), channel_id=1, source_target_pairs={{0,16},{16,32},{32,48},{48,64},{64,80},{80,96},{96,112},{1,17},{17... | collective-permute-start | bytes 3080 | tf_op jit(solution)/shard_map/ppermute | solution.py:18
  275.8 17.7 %collective-permute-start.30 = (f32[4,1,256]{2,0,1:T(4,128)S(1)}, f32[4,1,256]{2,0,1:T(4,128)S(1)}, u32[]{:S(2)}, u32[]{:S(2)}) collective-permute-start(f32[4,1,256]{2,0,1:T(4,128)S(1)} %get-tuple-element.90), channel_id=1, source_target_pairs={{0,16},{16,32},{32,48},{48,64},{64,80},{80,96},{96,112},{1,17},{17... | collective-permute-start | bytes 12296 | tf_op jit(solution)/shard_map/ppermute | solution.py:18
  284.7 11.5 %collective-permute-start.31 = (f32[4,1,256]{2,0,1:T(4,128)S(1)}, f32[4,1,256]{2,0,1:T(4,128)S(1)}, u32[]{:S(2)}, u32[]{:S(2)}) collective-permute-start(f32[4,1,256]{2,0,1:T(4,128)S(1)} %get-tuple-element.91), channel_id=1, source_target_pairs={{16,0},{32,16},{48,32},{64,48},{80,64},{96,80},{112,96},{17,1},{33... | collective-permute-start | bytes 12296 | tf_op jit(solution)/shard_map/ppermute | solution.py:21
  286.8 14.1 %collective-permute-start.68 = (f32[34,1]{1,0:T(8,128)S(1)}, f32[34,1]{1,0:T(8,128)S(1)}, u32[]{:S(2)}, u32[]{:S(2)}) collective-permute-start(f32[34,1]{1,0:T(8,128)S(1)} %get-tuple-element.152), channel_id=1, source_target_pairs={{0,1},{1,2},{2,3},{3,4},{4,5},{5,6},{6,7},{7,8},{8,9},{9,10},{10,1... | collective-permute-start | bytes 416 | tf_op jit(solution)/shard_map/ppermute | solution.py:18
  288.7 12.1 %collective-permute-start.69 = (f32[34,1]{1,0:T(8,128)S(1)}, f32[34,1]{1,0:T(8,128)S(1)}, u32[]{:S(2)}, u32[]{:S(2)}) collective-permute-start(f32[34,1]{1,0:T(8,128)S(1)} %get-tuple-element.151), channel_id=1, source_target_pairs={{1,0},{2,1},{3,2},{4,3},{5,4},{6,5},{7,6},{8,7},{9,8},{10,9},{11,1... | collective-permute-start | bytes 416 | tf_op jit(solution)/shard_map/ppermute | solution.py:21
  305.9 19.4 %collective-permute-start.42 = (f32[1,32,256]{2,0,1:T(1,128)S(1)}, f32[1,32,256]{2,0,1:T(1,128)S(1)}, u32[]{:S(2)}, u32[]{:S(2)}) collective-permute-start(f32[1,32,256]{2,0,1:T(1,128)S(1)} %get-tuple-element.135), channel_id=1, source_target_pairs={{0,128},{128,256},{256,384},{1,129},{129,257},{257,385},{2,130},{1... | collective-permute-start | bytes 98312 | tf_op jit(solution)/shard_map/ppermute | solution.py:18
  308.8 16.5 %collective-permute-start.43 = (f32[1,32,256]{2,0,1:T(1,128)S(1)}, f32[1,32,256]{2,0,1:T(1,128)S(1)}, u32[]{:S(2)}, u32[]{:S(2)}) collective-permute-start(f32[1,32,256]{2,0,1:T(1,128)S(1)} %get-tuple-element.136), channel_id=1, source_target_pairs={{128,0},{256,128},{384,256},{129,1},{257,129},{385,257},{130,2},{2... | collective-permute-start | bytes 98312 | tf_op jit(solution)/shard_map/ppermute | solution.py:21
  332.4 11.5 %collective-permute-start.45 = (f32[4,1,256]{2,0,1:T(4,128)S(1)}, f32[4,1,256]{2,0,1:T(4,128)S(1)}, u32[]{:S(2)}, u32[]{:S(2)}) collective-permute-start(f32[4,1,256]{2,0,1:T(4,128)S(1)} %get-tuple-element.89), channel_id=1, source_target_pairs={{16,0},{32,16},{48,32},{64,48},{80,64},{96,80},{112,96},{17,1},{33... | collective-permute-start | bytes 12296 | tf_op jit(solution)/shard_map/ppermute | solution.py:21
  344.1 17.5 %collective-permute-start.46 = (f32[4,34,1]{2,0,1:T(4,128)S(1)}, f32[4,34,1]{2,0,1:T(4,128)S(1)}, u32[]{:S(2)}, u32[]{:S(2)}) collective-permute-start(f32[4,34,1]{2,0,1:T(4,128)S(1)} %get-tuple-element.56), channel_id=1, source_target_pairs={{1,0},{2,1},{3,2},{4,3},{5,4},{6,5},{7,6},{8,7},{9,8},{10,9},{11,1... | collective-permute-start | bytes 1640 | tf_op jit(solution)/shard_map/ppermute | solution.py:21
  346.1 15.6 %collective-permute-start.47 = (f32[4,34,1]{2,0,1:T(4,128)S(1)}, f32[4,34,1]{2,0,1:T(4,128)S(1)}, u32[]{:S(2)}, u32[]{:S(2)}) collective-permute-start(f32[4,34,1]{2,0,1:T(4,128)S(1)} %get-tuple-element.57), channel_id=1, source_target_pairs={{0,1},{1,2},{2,3},{3,4},{4,5},{5,6},{6,7},{7,8},{8,9},{9,10},{10,1... | collective-permute-start | bytes 1640 | tf_op jit(solution)/shard_map/ppermute | solution.py:18
  372.1 11.5 %collective-permute-start.51 = (f32[4,1,256]{2,0,1:T(4,128)S(1)}, f32[4,1,256]{2,0,1:T(4,128)S(1)}, u32[]{:S(2)}, u32[]{:S(2)}) collective-permute-start(f32[4,1,256]{2,0,1:T(4,128)S(1)} %get-tuple-element.87), channel_id=1, source_target_pairs={{16,0},{32,16},{48,32},{64,48},{80,64},{96,80},{112,96},{17,1},{33... | collective-permute-start | bytes 12296 | tf_op jit(solution)/shard_map/ppermute | solution.py:21
  402.0 19.0 %collective-permute-start.56 = (f32[4,1,256]{2,0,1:T(4,128)S(1)}, f32[4,1,256]{2,0,1:T(4,128)S(1)}, u32[]{:S(2)}, u32[]{:S(2)}) collective-permute-start(f32[4,1,256]{2,0,1:T(4,128)S(1)} %get-tuple-element.84), channel_id=1, source_target_pairs={{0,16},{16,32},{32,48},{48,64},{64,80},{80,96},{96,112},{1,17},{17... | collective-permute-start | bytes 12296 | tf_op jit(solution)/shard_map/ppermute | solution.py:18
  404.0 17.1 %collective-permute-start.57 = (f32[4,1,256]{2,0,1:T(4,128)S(1)}, f32[4,1,256]{2,0,1:T(4,128)S(1)}, u32[]{:S(2)}, u32[]{:S(2)}) collective-permute-start(f32[4,1,256]{2,0,1:T(4,128)S(1)} %get-tuple-element.85), channel_id=1, source_target_pairs={{16,0},{32,16},{48,32},{64,48},{80,64},{96,80},{112,96},{17,1},{33... | collective-permute-start | bytes 12296 | tf_op jit(solution)/shard_map/ppermute | solution.py:21
  421.3 14.2 %collective-permute-start.58 = (f32[4,34,1]{2,0,1:T(4,128)S(1)}, f32[4,34,1]{2,0,1:T(4,128)S(1)}, u32[]{:S(2)}, u32[]{:S(2)}) collective-permute-start(f32[4,34,1]{2,0,1:T(4,128)S(1)} %get-tuple-element.52), channel_id=1, source_target_pairs={{1,0},{2,1},{3,2},{4,3},{5,4},{6,5},{7,6},{8,7},{9,8},{10,9},{11,1... | collective-permute-start | bytes 1640 | tf_op jit(solution)/shard_map/ppermute | solution.py:21
  423.2 12.3 %collective-permute-start.59 = (f32[4,34,1]{2,0,1:T(4,128)S(1)}, f32[4,34,1]{2,0,1:T(4,128)S(1)}, u32[]{:S(2)}, u32[]{:S(2)}) collective-permute-start(f32[4,34,1]{2,0,1:T(4,128)S(1)} %get-tuple-element.53), channel_id=1, source_target_pairs={{0,1},{1,2},{2,3},{3,4},{4,5},{5,6},{6,7},{7,8},{8,9},{9,10},{10,1... | collective-permute-start | bytes 1640 | tf_op jit(solution)/shard_map/ppermute | solution.py:18
  425.6 13.8 %collective-permute-start.94 = (f32[1,256]{1,0:T(1,128)S(1)}, f32[1,256]{1,0:T(1,128)S(1)}, u32[]{:S(2)}, u32[]{:S(2)}) collective-permute-start(f32[1,256]{1,0:T(1,128)S(1)} %get-tuple-element.159), channel_id=1, source_target_pairs={{0,16},{16,32},{32,48},{48,64},{64,80},{80,96},{96,112},{1,17},{17... | collective-permute-start | bytes 3080 | tf_op jit(solution)/shard_map/ppermute | solution.py:18
  445.1 17.6 %collective-permute-start.62 = (f32[4,1,256]{2,0,1:T(4,128)S(1)}, f32[4,1,256]{2,0,1:T(4,128)S(1)}, u32[]{:S(2)}, u32[]{:S(2)}) collective-permute-start(f32[4,1,256]{2,0,1:T(4,128)S(1)} %get-tuple-element.82), channel_id=1, source_target_pairs={{0,16},{16,32},{32,48},{48,64},{64,80},{80,96},{96,112},{1,17},{17... | collective-permute-start | bytes 12296 | tf_op jit(solution)/shard_map/ppermute | solution.py:18
  453.9 11.5 %collective-permute-start.63 = (f32[4,1,256]{2,0,1:T(4,128)S(1)}, f32[4,1,256]{2,0,1:T(4,128)S(1)}, u32[]{:S(2)}, u32[]{:S(2)}) collective-permute-start(f32[4,1,256]{2,0,1:T(4,128)S(1)} %get-tuple-element.83), channel_id=1, source_target_pairs={{16,0},{32,16},{48,32},{64,48},{80,64},{96,80},{112,96},{17,1},{33... | collective-permute-start | bytes 12296 | tf_op jit(solution)/shard_map/ppermute | solution.py:21
  455.9 14.1 %collective-permute-start.96 = (f32[34,1]{1,0:T(8,128)S(1)}, f32[34,1]{1,0:T(8,128)S(1)}, u32[]{:S(2)}, u32[]{:S(2)}) collective-permute-start(f32[34,1]{1,0:T(8,128)S(1)} %get-tuple-element.150), channel_id=1, source_target_pairs={{0,1},{1,2},{2,3},{3,4},{4,5},{5,6},{6,7},{7,8},{8,9},{9,10},{10,1... | collective-permute-start | bytes 416 | tf_op jit(solution)/shard_map/ppermute | solution.py:18
  457.8 12.1 %collective-permute-start.97 = (f32[34,1]{1,0:T(8,128)S(1)}, f32[34,1]{1,0:T(8,128)S(1)}, u32[]{:S(2)}, u32[]{:S(2)}) collective-permute-start(f32[34,1]{1,0:T(8,128)S(1)} %get-tuple-element.149), channel_id=1, source_target_pairs={{1,0},{2,1},{3,2},{4,3},{5,4},{6,5},{7,6},{8,7},{9,8},{10,9},{11,1... | collective-permute-start | bytes 416 | tf_op jit(solution)/shard_map/ppermute | solution.py:21
  475.1 19.4 %collective-permute-start.70 = (f32[1,32,256]{2,0,1:T(1,128)S(1)}, f32[1,32,256]{2,0,1:T(1,128)S(1)}, u32[]{:S(2)}, u32[]{:S(2)}) collective-permute-start(f32[1,32,256]{2,0,1:T(1,128)S(1)} %get-tuple-element.126), channel_id=1, source_target_pairs={{0,128},{128,256},{256,384},{1,129},{129,257},{257,385},{2,130},{1... | collective-permute-start | bytes 98312 | tf_op jit(solution)/shard_map/ppermute | solution.py:18
  478.2 16.2 %collective-permute-start.71 = (f32[1,32,256]{2,0,1:T(1,128)S(1)}, f32[1,32,256]{2,0,1:T(1,128)S(1)}, u32[]{:S(2)}, u32[]{:S(2)}) collective-permute-start(f32[1,32,256]{2,0,1:T(1,128)S(1)} %get-tuple-element.127), channel_id=1, source_target_pairs={{128,0},{256,128},{384,256},{129,1},{257,129},{385,257},{130,2},{2... | collective-permute-start | bytes 98312 | tf_op jit(solution)/shard_map/ppermute | solution.py:21
  501.6 11.5 %collective-permute-start.73 = (f32[4,1,256]{2,0,1:T(4,128)S(1)}, f32[4,1,256]{2,0,1:T(4,128)S(1)}, u32[]{:S(2)}, u32[]{:S(2)}) collective-permute-start(f32[4,1,256]{2,0,1:T(4,128)S(1)} %get-tuple-element.81), channel_id=1, source_target_pairs={{16,0},{32,16},{48,32},{64,48},{80,64},{96,80},{112,96},{17,1},{33... | collective-permute-start | bytes 12296 | tf_op jit(solution)/shard_map/ppermute | solution.py:21
  513.3 17.5 %collective-permute-start.74 = (f32[4,34,1]{2,0,1:T(4,128)S(1)}, f32[4,34,1]{2,0,1:T(4,128)S(1)}, u32[]{:S(2)}, u32[]{:S(2)}) collective-permute-start(f32[4,34,1]{2,0,1:T(4,128)S(1)} %get-tuple-element.48), channel_id=1, source_target_pairs={{1,0},{2,1},{3,2},{4,3},{5,4},{6,5},{7,6},{8,7},{9,8},{10,9},{11,1... | collective-permute-start | bytes 1640 | tf_op jit(solution)/shard_map/ppermute | solution.py:21
  515.2 15.6 %collective-permute-start.75 = (f32[4,34,1]{2,0,1:T(4,128)S(1)}, f32[4,34,1]{2,0,1:T(4,128)S(1)}, u32[]{:S(2)}, u32[]{:S(2)}) collective-permute-start(f32[4,34,1]{2,0,1:T(4,128)S(1)} %get-tuple-element.49), channel_id=1, source_target_pairs={{0,1},{1,2},{2,3},{3,4},{4,5},{5,6},{6,7},{7,8},{8,9},{9,10},{10,1... | collective-permute-start | bytes 1640 | tf_op jit(solution)/shard_map/ppermute | solution.py:18
  541.2 11.5 %collective-permute-start.79 = (f32[4,1,256]{2,0,1:T(4,128)S(1)}, f32[4,1,256]{2,0,1:T(4,128)S(1)}, u32[]{:S(2)}, u32[]{:S(2)}) collective-permute-start(f32[4,1,256]{2,0,1:T(4,128)S(1)} %get-tuple-element.79), channel_id=1, source_target_pairs={{16,0},{32,16},{48,32},{64,48},{80,64},{96,80},{112,96},{17,1},{33... | collective-permute-start | bytes 12296 | tf_op jit(solution)/shard_map/ppermute | solution.py:21
  571.2 19.0 %collective-permute-start.84 = (f32[4,1,256]{2,0,1:T(4,128)S(1)}, f32[4,1,256]{2,0,1:T(4,128)S(1)}, u32[]{:S(2)}, u32[]{:S(2)}) collective-permute-start(f32[4,1,256]{2,0,1:T(4,128)S(1)} %get-tuple-element.76), channel_id=1, source_target_pairs={{0,16},{16,32},{32,48},{48,64},{64,80},{80,96},{96,112},{1,17},{17... | collective-permute-start | bytes 12296 | tf_op jit(solution)/shard_map/ppermute | solution.py:18
  573.1 17.1 %collective-permute-start.85 = (f32[4,1,256]{2,0,1:T(4,128)S(1)}, f32[4,1,256]{2,0,1:T(4,128)S(1)}, u32[]{:S(2)}, u32[]{:S(2)}) collective-permute-start(f32[4,1,256]{2,0,1:T(4,128)S(1)} %get-tuple-element.77), channel_id=1, source_target_pairs={{16,0},{32,16},{48,32},{64,48},{80,64},{96,80},{112,96},{17,1},{33... | collective-permute-start | bytes 12296 | tf_op jit(solution)/shard_map/ppermute | solution.py:21
  590.4 14.2 %collective-permute-start.86 = (f32[4,34,1]{2,0,1:T(4,128)S(1)}, f32[4,34,1]{2,0,1:T(4,128)S(1)}, u32[]{:S(2)}, u32[]{:S(2)}) collective-permute-start(f32[4,34,1]{2,0,1:T(4,128)S(1)} %get-tuple-element.44), channel_id=1, source_target_pairs={{1,0},{2,1},{3,2},{4,3},{5,4},{6,5},{7,6},{8,7},{9,8},{10,9},{11,1... | collective-permute-start | bytes 1640 | tf_op jit(solution)/shard_map/ppermute | solution.py:21
  592.3 12.3 %collective-permute-start.87 = (f32[4,34,1]{2,0,1:T(4,128)S(1)}, f32[4,34,1]{2,0,1:T(4,128)S(1)}, u32[]{:S(2)}, u32[]{:S(2)}) collective-permute-start(f32[4,34,1]{2,0,1:T(4,128)S(1)} %get-tuple-element.45), channel_id=1, source_target_pairs={{0,1},{1,2},{2,3},{3,4},{4,5},{5,6},{6,7},{7,8},{8,9},{9,10},{10,1... | collective-permute-start | bytes 1640 | tf_op jit(solution)/shard_map/ppermute | solution.py:18
  594.8 13.8 %collective-permute-start.122 = (f32[1,256]{1,0:T(1,128)S(1)}, f32[1,256]{1,0:T(1,128)S(1)}, u32[]{:S(2)}, u32[]{:S(2)}) collective-permute-start(f32[1,256]{1,0:T(1,128)S(1)} %get-tuple-element.157), channel_id=1, source_target_pairs={{0,16},{16,32},{32,48},{48,64},{64,80},{80,96},{96,112},{1,17},{17... | collective-permute-start | bytes 3080 | tf_op jit(solution)/shard_map/ppermute | solution.py:18
  614.3 17.6 %collective-permute-start.90 = (f32[4,1,256]{2,0,1:T(4,128)S(1)}, f32[4,1,256]{2,0,1:T(4,128)S(1)}, u32[]{:S(2)}, u32[]{:S(2)}) collective-permute-start(f32[4,1,256]{2,0,1:T(4,128)S(1)} %get-tuple-element.74), channel_id=1, source_target_pairs={{0,16},{16,32},{32,48},{48,64},{64,80},{80,96},{96,112},{1,17},{17... | collective-permute-start | bytes 12296 | tf_op jit(solution)/shard_map/ppermute | solution.py:18
  623.0 11.5 %collective-permute-start.91 = (f32[4,1,256]{2,0,1:T(4,128)S(1)}, f32[4,1,256]{2,0,1:T(4,128)S(1)}, u32[]{:S(2)}, u32[]{:S(2)}) collective-permute-start(f32[4,1,256]{2,0,1:T(4,128)S(1)} %get-tuple-element.75), channel_id=1, source_target_pairs={{16,0},{32,16},{48,32},{64,48},{80,64},{96,80},{112,96},{17,1},{33... | collective-permute-start | bytes 12296 | tf_op jit(solution)/shard_map/ppermute | solution.py:21
  625.0 14.1 %collective-permute-start.124 = (f32[34,1]{1,0:T(8,128)S(1)}, f32[34,1]{1,0:T(8,128)S(1)}, u32[]{:S(2)}, u32[]{:S(2)}) collective-permute-start(f32[34,1]{1,0:T(8,128)S(1)} %get-tuple-element.148), channel_id=1, source_target_pairs={{0,1},{1,2},{2,3},{3,4},{4,5},{5,6},{6,7},{7,8},{8,9},{9,10},{10,1... | collective-permute-start | bytes 416 | tf_op jit(solution)/shard_map/ppermute | solution.py:18
  627.0 12.1 %collective-permute-start.125 = (f32[34,1]{1,0:T(8,128)S(1)}, f32[34,1]{1,0:T(8,128)S(1)}, u32[]{:S(2)}, u32[]{:S(2)}) collective-permute-start(f32[34,1]{1,0:T(8,128)S(1)} %get-tuple-element.147), channel_id=1, source_target_pairs={{1,0},{2,1},{3,2},{4,3},{5,4},{6,5},{7,6},{8,7},{9,8},{10,9},{11,1... | collective-permute-start | bytes 416 | tf_op jit(solution)/shard_map/ppermute | solution.py:21
  644.2 19.4 %collective-permute-start.98 = (f32[1,32,256]{2,0,1:T(1,128)S(1)}, f32[1,32,256]{2,0,1:T(1,128)S(1)}, u32[]{:S(2)}, u32[]{:S(2)}) collective-permute-start(f32[1,32,256]{2,0,1:T(1,128)S(1)} %get-tuple-element.117), channel_id=1, source_target_pairs={{0,128},{128,256},{256,384},{1,129},{129,257},{257,385},{2,130},{1... | collective-permute-start | bytes 98312 | tf_op jit(solution)/shard_map/ppermute | solution.py:18
  647.3 16.2 %collective-permute-start.99 = (f32[1,32,256]{2,0,1:T(1,128)S(1)}, f32[1,32,256]{2,0,1:T(1,128)S(1)}, u32[]{:S(2)}, u32[]{:S(2)}) collective-permute-start(f32[1,32,256]{2,0,1:T(1,128)S(1)} %get-tuple-element.118), channel_id=1, source_target_pairs={{128,0},{256,128},{384,256},{129,1},{257,129},{385,257},{130,2},{2... | collective-permute-start | bytes 98312 | tf_op jit(solution)/shard_map/ppermute | solution.py:21
  670.7 11.5 %collective-permute-start.101 = (f32[4,1,256]{2,0,1:T(4,128)S(1)}, f32[4,1,256]{2,0,1:T(4,128)S(1)}, u32[]{:S(2)}, u32[]{:S(2)}) collective-permute-start(f32[4,1,256]{2,0,1:T(4,128)S(1)} %get-tuple-element.73), channel_id=1, source_target_pairs={{16,0},{32,16},{48,32},{64,48},{80,64},{96,80},{112,96},{17,1},{33... | collective-permute-start | bytes 12296 | tf_op jit(solution)/shard_map/ppermute | solution.py:21
  682.4 17.5 %collective-permute-start.102 = (f32[4,34,1]{2,0,1:T(4,128)S(1)}, f32[4,34,1]{2,0,1:T(4,128)S(1)}, u32[]{:S(2)}, u32[]{:S(2)}) collective-permute-start(f32[4,34,1]{2,0,1:T(4,128)S(1)} %get-tuple-element.40), channel_id=1, source_target_pairs={{1,0},{2,1},{3,2},{4,3},{5,4},{6,5},{7,6},{8,7},{9,8},{10,9},{11,1... | collective-permute-start | bytes 1640 | tf_op jit(solution)/shard_map/ppermute | solution.py:21
  684.4 15.6 %collective-permute-start.103 = (f32[4,34,1]{2,0,1:T(4,128)S(1)}, f32[4,34,1]{2,0,1:T(4,128)S(1)}, u32[]{:S(2)}, u32[]{:S(2)}) collective-permute-start(f32[4,34,1]{2,0,1:T(4,128)S(1)} %get-tuple-element.41), channel_id=1, source_target_pairs={{0,1},{1,2},{2,3},{3,4},{4,5},{5,6},{6,7},{7,8},{8,9},{9,10},{10,1... | collective-permute-start | bytes 1640 | tf_op jit(solution)/shard_map/ppermute | solution.py:18
  710.4 11.5 %collective-permute-start.107 = (f32[4,1,256]{2,0,1:T(4,128)S(1)}, f32[4,1,256]{2,0,1:T(4,128)S(1)}, u32[]{:S(2)}, u32[]{:S(2)}) collective-permute-start(f32[4,1,256]{2,0,1:T(4,128)S(1)} %get-tuple-element.71), channel_id=1, source_target_pairs={{16,0},{32,16},{48,32},{64,48},{80,64},{96,80},{112,96},{17,1},{33... | collective-permute-start | bytes 12296 | tf_op jit(solution)/shard_map/ppermute | solution.py:21
  742.3 11.5 %collective-permute-start.113 = (f32[4,1,256]{2,0,1:T(4,128)S(1)}, f32[4,1,256]{2,0,1:T(4,128)S(1)}, u32[]{:S(2)}, u32[]{:S(2)}) collective-permute-start(f32[4,1,256]{2,0,1:T(4,128)S(1)} %get-tuple-element.69), channel_id=1, source_target_pairs={{16,0},{32,16},{48,32},{64,48},{80,64},{96,80},{112,96},{17,1},{33... | collective-permute-start | bytes 12296 | tf_op jit(solution)/shard_map/ppermute | solution.py:21
  774.9 11.5 %collective-permute-start.119 = (f32[4,1,256]{2,0,1:T(4,128)S(1)}, f32[4,1,256]{2,0,1:T(4,128)S(1)}, u32[]{:S(2)}, u32[]{:S(2)}) collective-permute-start(f32[4,1,256]{2,0,1:T(4,128)S(1)} %get-tuple-element.67), channel_id=1, source_target_pairs={{16,0},{32,16},{48,32},{64,48},{80,64},{96,80},{112,96},{17,1},{33... | collective-permute-start | bytes 12296 | tf_op jit(solution)/shard_map/ppermute | solution.py:21
  786.6 17.5 %collective-permute-start.120 = (f32[4,34,1]{2,0,1:T(4,128)S(1)}, f32[4,34,1]{2,0,1:T(4,128)S(1)}, u32[]{:S(2)}, u32[]{:S(2)}) collective-permute-start(f32[4,34,1]{2,0,1:T(4,128)S(1)} %get-tuple-element.34), channel_id=1, source_target_pairs={{1,0},{2,1},{3,2},{4,3},{5,4},{6,5},{7,6},{8,7},{9,8},{10,9},{11,1... | collective-permute-start | bytes 1640 | tf_op jit(solution)/shard_map/ppermute | solution.py:21
  788.5 15.6 %collective-permute-start.121 = (f32[4,34,1]{2,0,1:T(4,128)S(1)}, f32[4,34,1]{2,0,1:T(4,128)S(1)}, u32[]{:S(2)}, u32[]{:S(2)}) collective-permute-start(f32[4,34,1]{2,0,1:T(4,128)S(1)} %get-tuple-element.35), channel_id=1, source_target_pairs={{0,1},{1,2},{2,3},{3,4},{4,5},{5,6},{6,7},{7,8},{8,9},{9,10},{10,1... | collective-permute-start | bytes 1640 | tf_op jit(solution)/shard_map/ppermute | solution.py:18
  (78 other events, 1152.4 us)
